TPU v7x, 512 devices: a whole 4x8x8 slice. The times are simulated.
512 devices in a mesh: atom: 32 (over x, y_lo, core), chan: 8 (over z), rep: 2 (over y_hi).
Axes of the slice: x: 4, y: 8 (y_hi: 2, y_lo: 4; y = y_hi * 4 + y_lo), z: 8, core: 2. Of those that a mesh axis runs over, the one named last changes fastest.
Arguments:
- feats: bfloat16 [2, 128, 81, 512], P('rep', 'chan', None, 'atom'), may hold values from -6 to 6
- neighbors: int32 [2, 512, 32], P('rep', 'atom'), may hold values from 0 to 511, as said below
- counts: int32 [2, 512], P('rep', 'atom'), may hold values from 1 to 32, as said below
- radial: bfloat16 [2, 8, 16384], P('rep', None, 'atom'), may hold values from 2 to 6
- filter_weight: bfloat16 [8, 128, 81], P(None, 'chan'), may hold values from -0.3125 to 0.3125
- message_grad: bfloat16 [2, 128, 81, 16384], P('rep', 'chan', None, 'atom'), may hold values from -2 to 2
Outputs:
- feat_grad: float32 [2, 128, 81, 512], P('rep', 'chan', None, 'atom')
- radial_grad: float32 [2, 8, 16384], P('rep', None, 'atom')
- weight_grad: float32 [8, 128, 81], P(None, 'chan')
Inputs may be any that keep to these rules, and one draw needn't show every extreme that they name: `neighbors`: each source atom lies, counted cyclically, in the block of 16 consecutive atoms that holds its receiver or in one of the 2 such blocks on either side. `counts`: some atom of every crystal has all 32 slots valid.
All inputs are finite; a program needn't handle non-finite values.
Results may differ from a plain program's by a relative error of at most 0.0054.
Values may be sent and summed in bfloat16 or wider, within the bound.
No kernel may reach another device: no remote copies, remote signals or barrier semaphores. Data moves between devices by JAX's collectives and lax.ppermute only.
A program may use at most 64 MiB of HBM per device.

v0:
```python
import jax
import jax.numpy as jnp
from jax import lax
from jax.sharding import PartitionSpec as P

BASIS = 9
POINTS = 16
SLOTS = 32
REACH = 2
G = 81
SAMPLES = 256


def passed_along(value, axis, steps):
    count = lax.axis_size(axis)
    pairs = [(source, (source + steps) % count) for source in range(count)]
    return lax.ppermute(value, axis, pairs)


def basis_table():
    points = jnp.arange(POINTS, dtype=jnp.float32) * jnp.float32(2.0 * 3.141592653589793 / POINTS)
    degree_index = jnp.arange(BASIS, dtype=jnp.int32)
    frequency = ((degree_index + 1) // 2).astype(jnp.float32)
    angles = frequency[:, None] * points[None, :]
    root_two = jnp.sqrt(jnp.float32(2.0))
    single = jnp.where(
        degree_index[:, None] == 0,
        jnp.ones_like(angles),
        jnp.where(
            degree_index[:, None] % 2 == 1, root_two * jnp.cos(angles), root_two * jnp.sin(angles)
        ),
    )
    product = single[:, None, :, None] * single[None, :, None, :]
    return product.reshape(G, SAMPLES).astype(jnp.bfloat16)


def channel_terms(gathered, grad_c, weight_c, radial_e, valid_mask, synth_table, synth_rows):
    filter_edge = jnp.dot(weight_c.T, radial_e, preferred_element_type=jnp.float32).astype(
        jnp.bfloat16
    )
    feat_grid = jnp.dot(synth_rows, gathered, preferred_element_type=jnp.float32)
    filt_grid = jnp.dot(synth_rows, filter_edge, preferred_element_type=jnp.float32)
    weighted = (
        jnp.dot(synth_rows, grad_c, preferred_element_type=jnp.float32)
        * (valid_mask / SAMPLES)[None, :]
    )
    feat_side = (weighted * filt_grid).astype(jnp.bfloat16)
    filt_side = (weighted * feat_grid).astype(jnp.bfloat16)
    edge_grad = jnp.dot(synth_table, feat_side, preferred_element_type=jnp.float32).astype(
        jnp.bfloat16
    )
    filt_grad = jnp.dot(synth_table, filt_side, preferred_element_type=jnp.float32).astype(
        jnp.bfloat16
    )
    radial_part = jnp.dot(weight_c, filt_grad, preferred_element_type=jnp.float32)
    weight_part = jnp.dot(radial_e, filt_grad.T, preferred_element_type=jnp.float32)
    return (edge_grad, radial_part, weight_part)


def local(feats, neighbors, counts, radial, filter_weight, message_grad):
    synth_table = basis_table()
    synth_rows = synth_table.T
    atom_count = lax.axis_size("atom")
    position = lax.axis_index("atom")
    block_len = feats.shape[3]
    own_block = feats[0]
    chan_count = own_block.shape[0]
    pieces = []
    for offset in range(-REACH, REACH + 1):
        if offset == 0:
            pieces.append(own_block)
        else:
            pieces.append(passed_along(own_block, "atom", -offset))
    window = jnp.concatenate(pieces, axis=2)
    window_len = window.shape[2]
    sources = neighbors[0].reshape(-1)
    slot_index = (
        sources // block_len - position + REACH
    ) % atom_count * block_len + sources % block_len
    selector = (slot_index[None, :] == jnp.arange(window_len, dtype=jnp.int32)[:, None]).astype(
        jnp.bfloat16
    )
    gathered = jnp.dot(
        window.reshape(chan_count * G, window_len), selector, preferred_element_type=jnp.float32
    )
    gathered = gathered.astype(jnp.bfloat16).reshape(chan_count, G, -1)
    valid_mask = (
        (jnp.arange(SLOTS, dtype=jnp.int32)[None, :] < counts[0][:, None])
        .reshape(-1)
        .astype(jnp.float32)
    )
    radial_e = radial[0]

    def channel_step(running, inputs):
        gathered_c, grad_c, weight_c = inputs
        edge_grad, radial_part, weight_part = channel_terms(
            gathered_c, grad_c, weight_c, radial_e, valid_mask, synth_table, synth_rows
        )
        return (running + radial_part, (edge_grad, weight_part))

    radial_local, (edge_grads, weight_parts) = lax.scan(
        channel_step,
        jnp.zeros(radial_e.shape, jnp.float32),
        (gathered, message_grad[0], jnp.transpose(filter_weight, (1, 0, 2))),
    )
    window_grad = lax.dot_general(
        edge_grads.reshape(chan_count * G, -1),
        selector,
        (((1,), (1,)), ((), ())),
        preferred_element_type=jnp.float32,
    )

    def block_of(offset):
        return window_grad[:, (offset + REACH) * block_len : (offset + REACH + 1) * block_len]

    returned_sum = block_of(0)
    for offset in range(-REACH, REACH + 1):
        if offset != 0:
            returned_sum = returned_sum + passed_along(block_of(offset), "atom", offset)
    feat_grad = returned_sum.reshape(1, chan_count, G, block_len)
    radial_grad = lax.psum(radial_local, "chan")[None]
    weight_summed = lax.psum(jnp.transpose(weight_parts, (1, 0, 2)), ("atom", "rep"))
    weight_grad = weight_summed / (atom_count * block_len * lax.axis_size("rep"))
    return (feat_grad, radial_grad, weight_grad)


def solution(mesh):
    placed = (
        P("rep", "chan", None, "atom"),
        P("rep", "atom", None),
        P("rep", "atom"),
        P("rep", None, "atom"),
        P(None, "chan", None),
        P("rep", "chan", None, "atom"),
    )
    return jax.shard_map(
        local,
        mesh=mesh,
        in_specs=placed,
        out_specs=(P("rep", "chan", None, "atom"), P("rep", None, "atom"), P(None, "chan", None)),
        check_vma=False,
    )
```

profile of v0, /device:TPU:1, one launch (start us, length us, event | category | flops | bytes accessed | tf_op | source)
XLA Modules:
  0.0 431.3 jit_solution(14577033015070277945)
XLA Ops:
  0.6 4.0 collective-permute-start
  4.7 4.0 collective-permute-start.1
  8.7 4.5 %collective-permute-start.2 = (bf16[16,81,16]{1,2,0:T(8,128)(2,1)}, bf16[16,81,16]{1,2,0:T(8,128)(2,1)S(1)}, u32[]{:S(2)}, u32[]{:S(2)}) collective-permute-start(bf16[16,81,16]{1,2,0:T(8,128)(2,1)} %bitcast.107), channel_id=1, source_target_pairs={{0,496},{16,0},{32,16},{48,32},{64,48},{80,64},{96,80},{112,96},{1... | collective-permute-start | bytes 124424 | tf_op jit(solution)/shard_map/ppermute | solution.py:17
  13.2 7.6 %collective-permute-start.3 = (bf16[16,81,16]{1,2,0:T(8,128)(2,1)}, bf16[16,81,16]{1,2,0:T(8,128)(2,1)S(1)}, u32[]{:S(2)}, u32[]{:S(2)}) collective-permute-start(bf16[16,81,16]{1,2,0:T(8,128)(2,1)} %bitcast.108), channel_id=1, source_target_pairs={{0,480},{16,496},{32,0},{48,16},{64,32},{80,48},{96,64},{112,80},{... | collective-permute-start | bytes 124424 | tf_op jit(solution)/shard_map/ppermute | solution.py:17
  20.9 0.8 reshape_squeeze.3
  21.8 0.9 copy.17
  22.8 2.1 copy.26
  26.2 1.3 reshape.260
  27.6 61.8 %while.18 = (s32[]{:T(128)}, f32[8,512]{1,0:T(8,128)S(1)}, bf16[16,81,512]{2,1,0:T(8,128)(2,1)}, f32[16,8,81]{2,0,1:T(8,128)S(1)}, bf16[16,8,81]{2,1,0:T(8,128)(...) while((s32[]{:T(128)}, f32[8,512]{1,0:T(8,128)S(1)}, ...), condition=%wide.region_1.2_spmd.clone.clone.clone.clone, body=%wide.region_0.1_spmd.clone.clone.clone.clone.sunk | while | flops 108989952 | bytes 2697071 | solution.py:101
  28.7 1.1 fusion.98
  29.8 1.3 fusion.97
  32.5 1.1 fusion.98
  33.6 1.3 fusion.97
  36.4 1.1 fusion.98
  37.5 1.3 fusion.97
  40.3 1.1 fusion.98
  41.4 1.3 fusion.97
  44.1 1.1 fusion.98
  45.2 1.3 fusion.97
  48.0 1.1 fusion.98
  49.1 1.3 fusion.97
  51.9 1.1 fusion.98
  53.0 1.3 fusion.97
  55.7 1.1 fusion.98
  56.8 1.3 fusion.97
  59.6 1.1 fusion.98
  60.7 1.3 fusion.97
  63.5 1.1 fusion.98
  64.6 1.3 fusion.97
  67.3 1.1 fusion.98
  68.4 1.3 fusion.97
  71.2 1.1 fusion.98
  72.3 1.3 fusion.97
  75.0 1.1 fusion.98
  76.1 1.3 fusion.97
  78.9 1.1 fusion.98
  80.0 1.3 fusion.97
  82.8 1.1 fusion.98
  83.9 1.3 fusion.97
  86.6 1.1 fusion.98
  87.7 1.3 fusion.97
  89.4 1.6 reshape.261
  91.5 4.5 %collective-permute-start.4 = (f32[1296,16]{0,1:T(8,128)S(1)}, f32[1296,16]{0,1:T(8,128)S(1)}, u32[]{:S(2)}, u32[]{:S(2)}) collective-permute-start(f32[1296,16]{0,1:T(8,128)S(1)} %get-tuple-element.217), channel_id=1, source_target_pairs={{0,480},{16,496},{32,0},{48,16},{64,32},{80,48},{96,64},{112,80},{... | collective-permute-start | bytes 248840 | tf_op jit(solution)/shard_map/ppermute | solution.py:17
  96.0 5.1 %collective-permute-start.5 = (f32[1296,16]{0,1:T(8,128)S(1)}, f32[1296,16]{0,1:T(8,128)S(1)}, u32[]{:S(2)}, u32[]{:S(2)}) collective-permute-start(f32[1296,16]{0,1:T(8,128)S(1)} %get-tuple-element.220), channel_id=1, source_target_pairs={{0,496},{16,0},{32,16},{48,32},{64,48},{80,64},{96,80},{112,96},{1... | collective-permute-start | bytes 248840 | tf_op jit(solution)/shard_map/ppermute | solution.py:17
  101.1 1.9 collective-permute-start.6
  103.0 1.9 collective-permute-start.7
  104.9 295.5 %psum.15 = f32[8,16,81]{2,1,0:T(8,128)S(1)} all-reduce(f32[8,16,81]{2,1,0:T(8,128)S(1)} %bitcast.109), channel_id=1, replica_groups=mesh['atom'=32,'chan'=8,'rep'=2] {'atom','rep'}, use_global_device_ids=true, to_apply=%region_3.4 | all-reduce | flops 10368 | bytes 82944 | tf_op jit(solution)/shard_map/psum | solution.py:122
  401.0 29.3 %psum.14 = f32[1,8,512]{2,1,0:T(8,128)} all-reduce(f32[1,8,512]{2,1,0:T(8,128)S(1)} %bitcast.102), channel_id=1, replica_groups=mesh['atom'=32,'chan'=8,'rep'=2] {'chan'}, use_global_device_ids=true, to_apply=%region_2.3 | all-reduce | flops 4096 | bytes 32768 | tf_op jit(solution)/shard_map/psum | solution.py:121
  (204 shorter events, 26.0 us)
Async XLA Ops:
  0.6 24.3 %collective-permute-start = (bf16[16,81,16]{1,2,0:T(8,128)(2,1)}, bf16[16,81,16]{1,2,0:T(8,128)(2,1)S(1)}, u32[]{:S(2)}, u32[]{:S(2)}) collective-permute-start(bf16[16,81,16]{1,2,0:T(8,128)(2,1)} %bitcast.105), channel_id=1, source_target_pairs={{0,32},{16,48},{32,64},{48,80},{64,96},{80,112},{96,128},{112,144}... | collective-permute-start | bytes 124424 | tf_op jit(solution)/shard_map/ppermute | solution.py:17
  4.7 20.4 %collective-permute-start.1 = (bf16[16,81,16]{1,2,0:T(8,128)(2,1)}, bf16[16,81,16]{1,2,0:T(8,128)(2,1)S(1)}, u32[]{:S(2)}, u32[]{:S(2)}) collective-permute-start(bf16[16,81,16]{1,2,0:T(8,128)(2,1)} %bitcast.106), channel_id=1, source_target_pairs={{0,16},{16,32},{32,48},{48,64},{64,80},{80,96},{96,112},{112,128},... | collective-permute-start | bytes 124424 | tf_op jit(solution)/shard_map/ppermute | solution.py:17
  8.7 16.5 %collective-permute-start.2 = (bf16[16,81,16]{1,2,0:T(8,128)(2,1)}, bf16[16,81,16]{1,2,0:T(8,128)(2,1)S(1)}, u32[]{:S(2)}, u32[]{:S(2)}) collective-permute-start(bf16[16,81,16]{1,2,0:T(8,128)(2,1)} %bitcast.107), channel_id=1, source_target_pairs={{0,496},{16,0},{32,16},{48,32},{64,48},{80,64},{96,80},{112,96},{1... | collective-permute-start | bytes 124424 | tf_op jit(solution)/shard_map/ppermute | solution.py:17
  13.2 12.2 %collective-permute-start.3 = (bf16[16,81,16]{1,2,0:T(8,128)(2,1)}, bf16[16,81,16]{1,2,0:T(8,128)(2,1)S(1)}, u32[]{:S(2)}, u32[]{:S(2)}) collective-permute-start(bf16[16,81,16]{1,2,0:T(8,128)(2,1)} %bitcast.108), channel_id=1, source_target_pairs={{0,480},{16,496},{32,0},{48,16},{64,32},{80,48},{96,64},{112,80},{... | collective-permute-start | bytes 124424 | tf_op jit(solution)/shard_map/ppermute | solution.py:17
  22.6 2.2 copy-start.1
  26.2 1.4 copy-start
  26.2 1.4 copy-start.2
  91.5 338.8 %collective-permute-start.4 = (f32[1296,16]{0,1:T(8,128)S(1)}, f32[1296,16]{0,1:T(8,128)S(1)}, u32[]{:S(2)}, u32[]{:S(2)}) collective-permute-start(f32[1296,16]{0,1:T(8,128)S(1)} %get-tuple-element.217), channel_id=1, source_target_pairs={{0,480},{16,496},{32,0},{48,16},{64,32},{80,48},{96,64},{112,80},{... | collective-permute-start | bytes 248840 | tf_op jit(solution)/shard_map/ppermute | solution.py:17
  96.0 334.3 %collective-permute-start.5 = (f32[1296,16]{0,1:T(8,128)S(1)}, f32[1296,16]{0,1:T(8,128)S(1)}, u32[]{:S(2)}, u32[]{:S(2)}) collective-permute-start(f32[1296,16]{0,1:T(8,128)S(1)} %get-tuple-element.220), channel_id=1, source_target_pairs={{0,496},{16,0},{32,16},{48,32},{64,48},{80,64},{96,80},{112,96},{1... | collective-permute-start | bytes 248840 | tf_op jit(solution)/shard_map/ppermute | solution.py:17
  101.1 329.3 %collective-permute-start.6 = (f32[1296,16]{0,1:T(8,128)S(1)}, f32[1296,16]{0,1:T(8,128)S(1)}, u32[]{:S(2)}, u32[]{:S(2)}) collective-permute-start(f32[1296,16]{0,1:T(8,128)S(1)} %get-tuple-element.219), channel_id=1, source_target_pairs={{0,16},{16,32},{32,48},{48,64},{64,80},{80,96},{96,112},{112,128},... | collective-permute-start | bytes 248840 | tf_op jit(solution)/shard_map/ppermute | solution.py:17
  103.0 327.3 %collective-permute-start.7 = (f32[1296,16]{0,1:T(8,128)S(1)}, f32[1296,16]{0,1:T(8,128)S(1)}, u32[]{:S(2)}, u32[]{:S(2)}) collective-permute-start(f32[1296,16]{0,1:T(8,128)S(1)} %get-tuple-element.218), channel_id=1, source_target_pairs={{0,32},{16,48},{32,64},{48,80},{64,96},{80,112},{96,128},{112,144}... | collective-permute-start | bytes 248840 | tf_op jit(solution)/shard_map/ppermute | solution.py:17
where the time goes:
time: 436 us; the launch traced here: 431 us
  blocking collectives  325 us (75%)
  matrix products  51.8 us (12%)
  starting transfers between devices  33.6 us (8%)
  local copies, waits for them, and re-layouts  15.6 us (4%)
    psum x1, blocking collectives, local(): lax.psum(jnp.transpose(weight_parts, (1, 0, 2)), ('atom', 'rep'))  295 us
    ppermute x8, starting transfers between devices, passed_along(): return lax.ppermute(value, axis, pairs)  33.6 us
    psum x1, blocking collectives, local(): radial_grad = lax.psum(radial_local, 'chan')[None]  29.3 us
    dot_general x16, matrix products, channel_terms(): jnp.dot(synth_table, filt_side, preferred_element_type=jnp.float32)  21.3 us
    dot_general x16, matrix products, channel_terms(): jnp.dot(synth_table, feat_side, preferred_element_type=jnp.float32)  17.5 us
  transfers between devices with their start and end apart: 8, of which 0 were waited for; matrix products, arithmetic and copies ran while one was open for 1% of the time, Pallas kernels for 0%

commit v1 on v0

v1 whole, which is shorter than its diff:
```python
import functools

import jax
import jax.numpy as jnp
import numpy as np
from jax import lax
from jax.experimental import pallas as pl
from jax.experimental.pallas import tpu as pltpu
from jax.sharding import PartitionSpec as P

BASIS = 9
POINTS = 16
SLOTS = 32
REACH = 2
BLOCKS = 2 * REACH + 1
G = 81
SAMPLES = 256
WINDOW = 128

VMEM = pl.BlockSpec(memory_space=pltpu.VMEM)


def passed_along(value, axis, steps):
    count = lax.axis_size(axis)
    pairs = [(source, (source + steps) % count) for source in range(count)]
    return lax.ppermute(value, axis, pairs)


def basis_table():
    points = np.arange(POINTS) * (2.0 * np.pi / POINTS)
    rows = [np.ones(POINTS)]
    for k in range(1, BASIS // 2 + 1):
        rows.append(np.sqrt(2.0) * np.cos(k * points))
        rows.append(np.sqrt(2.0) * np.sin(k * points))
    single = np.stack(rows).astype(np.float32)
    product = single[:, None, :, None] * single[None, :, None, :]
    return product.reshape(G, SAMPLES).astype(jnp.bfloat16)


def dot(a, b):
    return jnp.dot(a, b, preferred_element_type=jnp.float32)


def dot_nt(a, b):
    return lax.dot_general(a, b, (((1,), (1,)), ((), ())), preferred_element_type=jnp.float32)


def selector(neighbors_ref, counts_ref, block_len, edges):
    position = lax.axis_index("atom")
    atom_count = lax.axis_size("atom")
    sources = neighbors_ref[...]
    block = lax.rem(
        lax.div(sources, block_len) - position + (REACH + atom_count), jnp.int32(atom_count)
    )
    slot = (block * block_len + lax.rem(sources, block_len)).astype(jnp.bfloat16)
    edge = lax.broadcasted_iota(jnp.int32, (SLOTS, edges), 1)
    spread = (edge % SLOTS == lax.broadcasted_iota(jnp.int32, (SLOTS, edges), 0)).astype(jnp.bfloat16)
    edge = lax.broadcasted_iota(jnp.int32, (block_len, edges), 1)
    mine = edge // SLOTS == lax.broadcasted_iota(jnp.int32, (block_len, edges), 0)
    slot_row = jnp.sum(jnp.where(mine, dot(slot, spread), 0.0), axis=0, keepdims=True)
    counts = jnp.broadcast_to(counts_ref[...], (8, block_len)).astype(jnp.bfloat16)
    count_row = dot(counts, mine.astype(jnp.bfloat16))[:1]
    in_row = (lax.broadcasted_iota(jnp.int32, (1, edges), 1) % SLOTS).astype(jnp.float32)
    slot_row = jnp.where(in_row < count_row, slot_row, -1.0)
    window = lax.broadcasted_iota(jnp.int32, (WINDOW, edges), 0).astype(jnp.float32)
    return (window == slot_row).astype(jnp.bfloat16)


def split(value, axis):
    high = value.astype(jnp.bfloat16)
    low = (value - high.astype(jnp.float32)).astype(jnp.bfloat16)
    half = value.shape[axis] // 2
    first = lax.broadcasted_iota(jnp.int32, value.shape, axis) < half
    return jnp.where(first, high.astype(jnp.float32), low.astype(jnp.float32)).astype(jnp.bfloat16)


def filter_side(
    grad_ref, weight_ref, neighbors_ref, counts_ref, radial_ref, table_ref, rows_ref,
    *refs,
):
    blocks = refs[:BLOCKS]
    weight_out, radial_out = refs[BLOCKS : BLOCKS + 2]
    sel_ref, window_ref, total_ref, moments_ref = refs[BLOCKS + 2 :]
    chan_count, _, edges = grad_ref.shape
    block_len = blocks[0].shape[1]
    sel_ref[...] = selector(neighbors_ref, counts_ref, block_len, edges)
    window_ref[...] = jnp.zeros_like(window_ref)
    total_ref[...] = jnp.zeros_like(total_ref)

    @pl.loop(0, chan_count)
    def _(c):
        for j in range(BLOCKS):
            window_ref[j * block_len : (j + 1) * block_len, :] = blocks[j][c]
        window_grid = dot_nt(rows_ref[...], window_ref[...]).astype(jnp.bfloat16)
        weighted = dot(rows_ref[...], grad_ref[c])
        feat_grid = dot(window_grid, sel_ref[...])
        filt_side = (weighted * feat_grid).astype(jnp.bfloat16)
        weight_grid = split(dot(weight_ref[c], table_ref[...]), 0)
        total_ref[...] += dot(weight_grid, filt_side)
        moments_ref[c] = dot_nt(radial_ref[...], filt_side)

    degrees = radial_ref.shape[0]
    radial_sum = (total_ref[:degrees] + total_ref[degrees:]) * (1.0 / SAMPLES)
    for j in range(radial_out.shape[0]):
        radial_out[j] = radial_sum
    moments = moments_ref[...].reshape(chan_count * degrees, SAMPLES)
    high = moments.astype(jnp.bfloat16)
    low = (moments - high.astype(jnp.float32)).astype(jnp.bfloat16)
    weight = dot_nt(high, table_ref[...]) + dot_nt(low, table_ref[...])
    weight_out[...] = weight * (1.0 / SAMPLES)


def feature_side(
    grad_ref, weight_ref, neighbors_ref, counts_ref, radial_ref, table_ref, rows_ref,
    *refs,
):
    outs = refs[:BLOCKS]
    sel_ref = refs[BLOCKS]
    chan_count, _, edges = grad_ref.shape
    block_len = outs[0].shape[1]
    sel_ref[...] = selector(neighbors_ref, counts_ref, block_len, edges)
    radial = jnp.concatenate([radial_ref[...]] * 2, axis=0)

    @pl.loop(0, chan_count)
    def _(c):
        weight_grid = split(dot_nt(rows_ref[...], weight_ref[c]), 1)
        filt_grid = dot(weight_grid, radial)
        weighted = dot(rows_ref[...], grad_ref[c])
        feat_side = (weighted * filt_grid).astype(jnp.bfloat16)
        window_grid = dot_nt(sel_ref[...], feat_side).astype(jnp.bfloat16)
        window_grad = dot(window_grid, rows_ref[...]) * (1.0 / SAMPLES)
        for j in range(BLOCKS):
            outs[j][c] = window_grad[j * block_len : (j + 1) * block_len, :]


def local(feats, neighbors, counts, radial, filter_weight, message_grad):
    table = basis_table()
    rows = jnp.asarray(np.ascontiguousarray(table.T))
    table = jnp.asarray(table)
    atom_count = lax.axis_size("atom")
    chan_devices = lax.axis_size("chan")
    _, chan_count, _, block_len = feats.shape
    degrees, edges = radial.shape[1:]
    own_block = jnp.transpose(feats[0], (0, 2, 1))
    halo = [
        own_block if offset == 0 else passed_along(own_block, "atom", -offset)
        for offset in range(-REACH, REACH + 1)
    ]
    weight = jnp.transpose(filter_weight, (1, 0, 2))
    weight = jnp.concatenate([weight, weight], axis=1)
    common = (message_grad[0], weight, neighbors[0], counts, radial[0], table, rows)
    weight_part, radial_part = pl.pallas_call(
        filter_side,
        out_shape=(
            jax.ShapeDtypeStruct((chan_count * degrees, G), jnp.float32),
            jax.ShapeDtypeStruct((chan_devices, degrees, edges), jnp.float32),
        ),
        in_specs=[VMEM] * (len(common) + BLOCKS),
        out_specs=(VMEM, VMEM),
        scratch_shapes=[
            pltpu.VMEM((WINDOW, edges), jnp.bfloat16),
            pltpu.VMEM((WINDOW, G), jnp.bfloat16),
            pltpu.VMEM((2 * degrees, edges), jnp.float32),
            pltpu.VMEM((chan_count, degrees, SAMPLES), jnp.float32),
        ],
        cost_estimate=pl.CostEstimate(flops=6 * 10**9, bytes_accessed=4 * 10**6, transcendentals=0),
        name="filter_side",
    )(*common, *halo)

    group = ("atom", "rep")
    members = lax.axis_size(group)
    pieces = lax.all_to_all(weight_part.reshape(members, -1, G), group, 0, 0, tiled=True)
    radial_parts = lax.all_to_all(radial_part, "chan", 0, 0, tiled=True)

    window_grads = pl.pallas_call(
        feature_side,
        out_shape=[jax.ShapeDtypeStruct((chan_count, block_len, G), jnp.float32)] * BLOCKS,
        in_specs=[VMEM] * len(common),
        out_specs=[VMEM] * BLOCKS,
        scratch_shapes=[pltpu.VMEM((WINDOW, edges), jnp.bfloat16)],
        cost_estimate=pl.CostEstimate(flops=6 * 10**9, bytes_accessed=4 * 10**6, transcendentals=0),
        name="feature_side",
    )(*common)

    piece = jnp.sum(pieces, axis=0, keepdims=True) / (atom_count * block_len * lax.axis_size("rep"))
    weight_grad = lax.all_to_all(jnp.broadcast_to(piece, pieces.shape), group, 0, 0, tiled=True)
    weight_grad = jnp.transpose(weight_grad.reshape(chan_count, degrees, G), (1, 0, 2))
    feat_grad = window_grads[REACH]
    for offset in range(-REACH, REACH + 1):
        if offset != 0:
            feat_grad = feat_grad + passed_along(window_grads[offset + REACH], "atom", offset)
    feat_grad = jnp.transpose(feat_grad, (0, 2, 1))[None]
    radial_grad = jnp.sum(radial_parts, axis=0, keepdims=True)
    return (feat_grad, radial_grad, weight_grad)


def solution(mesh):
    placed = (
        P("rep", "chan", None, "atom"),
        P("rep", "atom", None),
        P("rep", "atom"),
        P("rep", None, "atom"),
        P(None, "chan", None),
        P("rep", "chan", None, "atom"),
    )
    return jax.shard_map(
        local,
        mesh=mesh,
        in_specs=placed,
        out_specs=(P("rep", "chan", None, "atom"), P("rep", None, "atom"), P(None, "chan", None)),
        check_vma=False,
    )
```

time: 436 us -> 110 us (0.25)
  blocking collectives: 325 us -> 17.5 us
  matrix products: 51.8 us -> 0 us
  Pallas kernels: 0 us -> 26.2 us
  starting transfers between devices: 33.6 us -> 50.7 us
  local copies, waits for them, and re-layouts: 15.6 us -> 5.25 us
  waiting for transfers between devices: 0.02 us -> 5.5 us
    psum x2 -> x0, blocking collectives: 325 us -> none  [the longest x1 295 us: local(): lax.psum(jnp.transpose(weight_parts, (1, 0, 2)), ('atom', 'rep'))]
    dot_general x98 -> x0, matrix products: 51.8 us -> none  [the longest x16 21.3 us: channel_terms(): jnp.dot(synth_table, filt_side, preferred_element_type=jnp.float32)]
    pallas_call x0 -> x2, Pallas kernels: none -> 26.2 us  [the longest x1 14 us: local(): pl.pallas_call(feature_side, out_shape=[jax.ShapeDtypeStruct((chan_count,...]
    all_to_all x0 -> x1, blocking collectives: none -> 17.5 us  [local(): lax.all_to_all(jnp.broadcast_to(piece, pieces.shape), group, 0, 0, tiled=...]
    all_to_all x0 -> x2, starting transfers between devices: none -> 15.6 us  [the longest x1 8.07 us: local(): radial_parts = lax.all_to_all(radial_part, 'chan', 0, 0, tiled=True)]
    convert_element_type x32 -> x0, local copies, waits for them, and re-layouts: 6.78 us -> none  [the longest x16 5.49 us: basis_table(): return product.reshape(G, SAMPLES).astype(jnp.bfloat16)]
    all_to_all x0 -> x2, waiting for transfers between devices: none -> 5.47 us  [the longest x1 5.47 us: local(): radial_parts = lax.all_to_all(radial_part, 'chan', 0, 0, tiled=True)]
  transfers between devices with their start and end apart: 8 -> 10, of which waited for: 0 -> 1; matrix products, arithmetic and copies ran while one was open for 1% -> 6% of each run, Pallas kernels for 0% -> 13%
where the time goes in v1:
time: 110 us; the launch traced here: 109 us
  starting transfers between devices  50.7 us (46%)
  Pallas kernels  26.2 us (24%)
  blocking collectives  17.5 us (16%)
  waiting for transfers between devices  5.5 us (5%)
  local copies, waits for them, and re-layouts  5.25 us (5%)
  other arithmetic  2.95 us (3%)
    ppermute x8, starting transfers between devices, passed_along(): return lax.ppermute(value, axis, pairs)  35.1 us
    all_to_all x1, blocking collectives, local(): lax.all_to_all(jnp.broadcast_to(piece, pieces.shape), group, 0, 0, tiled=...  17.5 us
    pallas_call x1, Pallas kernels, local(): pl.pallas_call(feature_side, out_shape=[jax.ShapeDtypeStruct((chan_count,...  14 us
    pallas_call x1, Pallas kernels, local(): pl.pallas_call(filter_side, out_shape=(jax.ShapeDtypeStruct((chan_count *...  12.2 us
    all_to_all x1, starting transfers between devices, local(): radial_parts = lax.all_to_all(radial_part, 'chan', 0, 0, tiled=True)  8.07 us
    all_to_all x1, starting transfers between devices, local(): lax.all_to_all(weight_part.reshape(members, -1, G), group, 0, 0, tiled=True)  7.54 us
    all_to_all x1, waiting for transfers between devices, local(): radial_parts = lax.all_to_all(radial_part, 'chan', 0, 0, tiled=True)  5.47 us
    unnamed x11, local copies, waits for them, and re-layouts  5.23 us
  transfers between devices with their start and end apart: 10, of which 1 were waited for; matrix products, arithmetic and copies ran while one was open for 6% of the time, Pallas kernels for 13%

profile of v1, /device:TPU:1, one launch (start us, length us, event | category | flops | bytes accessed | tf_op | source)
XLA Modules:
  0.0 108.9 jit_solution(12638515693879739779)
XLA Ops:
  0.6 4.0 %collective-permute-start.4 = (bf16[16,16,81]{2,1,0:T(8,128)(2,1)}, bf16[16,16,81]{2,1,0:T(8,128)(2,1)S(1)}, u32[]{:S(2)}, u32[]{:S(2)}) collective-permute-start(bf16[16,16,81]{2,1,0:T(8,128)(2,1)} %bitcast.26), channel_id=1, source_target_pairs={{0,32},{16,48},{32,64},{48,80},{64,96},{80,112},{96,128},{112,144}... | collective-permute-start | bytes 124424 | tf_op jit(solution)/shard_map/ppermute | solution.py:26
  4.7 4.0 %collective-permute-start.5 = (bf16[16,16,81]{2,1,0:T(8,128)(2,1)}, bf16[16,16,81]{2,1,0:T(8,128)(2,1)S(1)}, u32[]{:S(2)}, u32[]{:S(2)}) collective-permute-start(bf16[16,16,81]{2,1,0:T(8,128)(2,1)} %bitcast.27), channel_id=1, source_target_pairs={{0,16},{16,32},{32,48},{48,64},{64,80},{80,96},{96,112},{112,128},... | collective-permute-start | bytes 124424 | tf_op jit(solution)/shard_map/ppermute | solution.py:26
  8.7 4.5 %collective-permute-start.6 = (bf16[16,16,81]{2,1,0:T(8,128)(2,1)}, bf16[16,16,81]{2,1,0:T(8,128)(2,1)S(1)}, u32[]{:S(2)}, u32[]{:S(2)}) collective-permute-start(bf16[16,16,81]{2,1,0:T(8,128)(2,1)} %bitcast.28), channel_id=1, source_target_pairs={{0,496},{16,0},{32,16},{48,32},{64,48},{80,64},{96,80},{112,96},{1... | collective-permute-start | bytes 124424 | tf_op jit(solution)/shard_map/ppermute | solution.py:26
  13.2 7.6 %collective-permute-start.7 = (bf16[16,16,81]{2,1,0:T(8,128)(2,1)}, bf16[16,16,81]{2,1,0:T(8,128)(2,1)S(1)}, u32[]{:S(2)}, u32[]{:S(2)}) collective-permute-start(bf16[16,16,81]{2,1,0:T(8,128)(2,1)} %bitcast.29), channel_id=1, source_target_pairs={{0,480},{16,496},{32,0},{48,16},{64,32},{80,48},{96,64},{112,80},{... | collective-permute-start | bytes 124424 | tf_op jit(solution)/shard_map/ppermute | solution.py:26
  20.8 0.8 copy.19
  21.6 0.6 pad_maximum_fusion.weight_ref
  22.2 3.2 %copy.18 = bf16[1,16,81,512]{3,2,1,0:T(8,128)(2,1)} copy(bf16[1,16,81,512]{3,1,2,0:T(8,128)(2,1)} %param.13) | data formatting | bytes 2654208 | tf_op args[5]
  25.4 0.0 collective-permute-done.4.refs_0_
  25.4 0.0 copy-start
  25.4 0.0 collective-permute-done.5.refs_1_
  25.4 0.0 copy-start.1
  25.4 0.0 collective-permute-done.6.refs_3_
  25.4 0.0 copy-start.2
  25.4 0.0 collective-permute-done.7.refs_4_
  25.5 0.0 copy-start.3
  25.5 0.6 copy-done
  26.0 0.0 copy-done.1
  26.0 0.0 copy-done.2
  26.1 0.0 copy-done.3
  26.1 12.2 %filter_side.1 = (f32[128,81]{1,0:T(8,128)}, f32[8,8,512]{2,1,0:T(8,128)}) custom-call(bf16[16,81,512]{2,1,0:T(8,128)(2,1)} %bitcast.20, bf16[16,16,81]{2,1,0:T(8,128)(2,1)} %pad_maximum_fusion.weight_ref, s32[16,32]{1,0:T(8,128)} %bitcast.31, s32[1,16]{1,0:T(1,128)} %counts_ref.3, bf16[8,512]{1,0:T(8,128)(2,1)} %bitcast.33, ...), custom_call_target="tpu_custom_call" | custom-call | flops 6000000000 | bytes 4000000 | tf_op jit(solution)/shard_map/filter_side/pallas_call | solution.py:152
  38.3 7.5 %all-to-all-start.1 = ((f32[64,2,81]{2,1,0:T(2,128)}), f32[64,2,81]{2,1,0:T(2,128)S(1)}, u32[]{:S(2)}, u32[]{:S(2)}) async-start(f32[64,2,81]{2,1,0:T(2,128)} %bitcast.24), calls=%async_computation.1 | async-start | bytes 131072 | tf_op jit(solution)/shard_map/all_to_all | solution.py:172
  45.8 14.0 %feature_side.1 = (f32[16,16,81]{2,1,0:T(8,128)}, f32[16,16,81]{2,1,0:T(8,128)}, f32[16,16,81]{2,1,0:T(8,128)}, f32[16,16,81]{2,1,0:T(8,128)}, f32[16,16,81]{2,1,0:T(8,128)}) custom-call(bf16[16,81,512]{2,1,0:T(8,128)(2,1)} %bitcast.21, bf16[16,16,81]{2,1,0:T(8,128)(2,1)} %pad_maximum_fusion.weight_ref, s32[16,32]{1,0:T(8,128)} %bitcast.32, ...), custom_call_target="tpu_custom_call" | custom-call | flops 6000000000 | bytes 4000000 | tf_op jit(solution)/shard_map/feature_side/pallas_call | solution.py:175
  59.8 7.5 %collective-permute-start = (f32[16,16,81]{2,1,0:T(8,128)}, f32[16,16,81]{2,1,0:T(8,128)S(1)}, u32[]{:S(2)}, u32[]{:S(2)}) collective-permute-start(f32[16,16,81]{2,1,0:T(8,128)} %get-tuple-element.11), channel_id=1, source_target_pairs={{0,480},{16,496},{32,0},{48,16},{64,32},{80,48},{96,64},{112,80},{... | collective-permute-start | bytes 248840 | tf_op jit(solution)/shard_map/ppermute | solution.py:26
  67.3 2.6 %collective-permute-start.1 = (f32[16,16,81]{2,1,0:T(8,128)}, f32[16,16,81]{2,1,0:T(8,128)S(1)}, u32[]{:S(2)}, u32[]{:S(2)}) collective-permute-start(f32[16,16,81]{2,1,0:T(8,128)} %get-tuple-element.12), channel_id=1, source_target_pairs={{0,496},{16,0},{32,16},{48,32},{64,48},{80,64},{96,80},{112,96},{1... | collective-permute-start | bytes 248840 | tf_op jit(solution)/shard_map/ppermute | solution.py:26
  69.9 3.0 %collective-permute-start.2 = (f32[16,16,81]{2,1,0:T(8,128)}, f32[16,16,81]{2,1,0:T(8,128)S(1)}, u32[]{:S(2)}, u32[]{:S(2)}) collective-permute-start(f32[16,16,81]{2,1,0:T(8,128)} %get-tuple-element.13), channel_id=1, source_target_pairs={{0,16},{16,32},{32,48},{48,64},{64,80},{80,96},{96,112},{112,128},... | collective-permute-start | bytes 248840 | tf_op jit(solution)/shard_map/ppermute | solution.py:26
  72.9 1.9 %collective-permute-start.3 = (f32[16,16,81]{2,1,0:T(8,128)}, f32[16,16,81]{2,1,0:T(8,128)S(1)}, u32[]{:S(2)}, u32[]{:S(2)}) collective-permute-start(f32[16,16,81]{2,1,0:T(8,128)} %get-tuple-element.14), channel_id=1, source_target_pairs={{0,32},{16,48},{32,64},{48,80},{64,96},{80,112},{96,128},{112,144}... | collective-permute-start | bytes 248840 | tf_op jit(solution)/shard_map/ppermute | solution.py:26
  74.8 0.0 all-to-all-done.1
  74.8 0.1 reduce_sum.19
  74.9 17.5 %all_to_all.15 = f32[64,2,81]{2,1,0:T(2,128)S(1)} all-to-all(f32[64,2,81]{2,1,0:T(2,128)S(1)} %broadcast_in_dim.14), channel_id=1, replica_groups=mesh['atom'=32,'chan'=8,'rep'=2] {'atom','rep'}, dimensions={0} | all-to-all | bytes 82944 | tf_op jit(solution)/shard_map/all_to_all | solution.py:186
  92.5 8.1 %all-to-all-start = ((f32[8,8,512]{2,1,0:T(8,128)}), f32[8,8,512]{2,1,0:T(8,128)S(1)}, u32[]{:S(2)}, u32[]{:S(2)}) async-start(f32[8,8,512]{2,1,0:T(8,128)} %get-tuple-element.15), calls=%async_computation | async-start | bytes 262144 | tf_op jit(solution)/shard_map/all_to_all | solution.py:173
  100.5 0.0 collective-permute-done
  100.5 0.0 collective-permute-done.1
  100.6 0.0 collective-permute-done.2
  100.6 0.0 collective-permute-done.3
  100.6 1.6 %add_bitcast_fusion = f32[1,16,81,16]{2,3,1,0:T(8,128)} fusion(f32[16,16,81]{2,1,0:T(8,128)S(1)} %collective-permute-done.3, f32[16,16,81]{2,1,0:T(8,128)S(1)} %collective-permute-done.2, f32[16,16,81]{2,1,0:T(8,128)S(1)} %collective-permute-done.1, f32[16,16,81]{2,1,0:T(8,128)} %get-tuple-element.10, f32[16,16,81]{2,1,0:T(8,128)S(1)} %collective-permute-done), kind=kLoop, calls=%fused_computation.1 | loop fusion | flops 82944 | bytes 497664 | tf_op jit(solution)/shard_map/broadcast_in_dim | solution.py:192
  102.2 0.6 copy.15
  102.8 5.5 %all-to-all-done = f32[8,8,512]{2,1,0:T(8,128)S(1)} async-done(((f32[8,8,512]{2,1,0:T(8,128)}), f32[8,8,512]{2,1,0:T(8,128)S(1)}, u32[]{:S(2)}, u32[]{:S(2)}) %all-to-all-start) | async-done | bytes 131104 | tf_op jit(solution)/shard_map/all_to_all | solution.py:173
  108.3 0.6 reduce_sum.18
  (2 shorter events, 0.0 us)
Async XLA Ops:
  0.6 24.8 %collective-permute-start.4 = (bf16[16,16,81]{2,1,0:T(8,128)(2,1)}, bf16[16,16,81]{2,1,0:T(8,128)(2,1)S(1)}, u32[]{:S(2)}, u32[]{:S(2)}) collective-permute-start(bf16[16,16,81]{2,1,0:T(8,128)(2,1)} %bitcast.26), channel_id=1, source_target_pairs={{0,32},{16,48},{32,64},{48,80},{64,96},{80,112},{96,128},{112,144}... | collective-permute-start | bytes 124424 | tf_op jit(solution)/shard_map/ppermute | solution.py:26
  4.7 20.7 %collective-permute-start.5 = (bf16[16,16,81]{2,1,0:T(8,128)(2,1)}, bf16[16,16,81]{2,1,0:T(8,128)(2,1)S(1)}, u32[]{:S(2)}, u32[]{:S(2)}) collective-permute-start(bf16[16,16,81]{2,1,0:T(8,128)(2,1)} %bitcast.27), channel_id=1, source_target_pairs={{0,16},{16,32},{32,48},{48,64},{64,80},{80,96},{96,112},{112,128},... | collective-permute-start | bytes 124424 | tf_op jit(solution)/shard_map/ppermute | solution.py:26
  8.7 16.7 %collective-permute-start.6 = (bf16[16,16,81]{2,1,0:T(8,128)(2,1)}, bf16[16,16,81]{2,1,0:T(8,128)(2,1)S(1)}, u32[]{:S(2)}, u32[]{:S(2)}) collective-permute-start(bf16[16,16,81]{2,1,0:T(8,128)(2,1)} %bitcast.28), channel_id=1, source_target_pairs={{0,496},{16,0},{32,16},{48,32},{64,48},{80,64},{96,80},{112,96},{1... | collective-permute-start | bytes 124424 | tf_op jit(solution)/shard_map/ppermute | solution.py:26
  13.2 12.2 %collective-permute-start.7 = (bf16[16,16,81]{2,1,0:T(8,128)(2,1)}, bf16[16,16,81]{2,1,0:T(8,128)(2,1)S(1)}, u32[]{:S(2)}, u32[]{:S(2)}) collective-permute-start(bf16[16,16,81]{2,1,0:T(8,128)(2,1)} %bitcast.29), channel_id=1, source_target_pairs={{0,480},{16,496},{32,0},{48,16},{64,32},{80,48},{96,64},{112,80},{... | collective-permute-start | bytes 124424 | tf_op jit(solution)/shard_map/ppermute | solution.py:26
  25.4 0.6 copy-start
  25.4 0.6 copy-start.1
  25.4 0.6 copy-start.2
  25.5 0.6 copy-start.3
  38.3 36.5 %all-to-all-start.1 = ((f32[64,2,81]{2,1,0:T(2,128)}), f32[64,2,81]{2,1,0:T(2,128)S(1)}, u32[]{:S(2)}, u32[]{:S(2)}) async-start(f32[64,2,81]{2,1,0:T(2,128)} %bitcast.24), calls=%async_computation.1 | async-start | bytes 131072 | tf_op jit(solution)/shard_map/all_to_all | solution.py:172
  59.8 40.7 %collective-permute-start = (f32[16,16,81]{2,1,0:T(8,128)}, f32[16,16,81]{2,1,0:T(8,128)S(1)}, u32[]{:S(2)}, u32[]{:S(2)}) collective-permute-start(f32[16,16,81]{2,1,0:T(8,128)} %get-tuple-element.11), channel_id=1, source_target_pairs={{0,480},{16,496},{32,0},{48,16},{64,32},{80,48},{96,64},{112,80},{... | collective-permute-start | bytes 248840 | tf_op jit(solution)/shard_map/ppermute | solution.py:26
  67.3 33.3 %collective-permute-start.1 = (f32[16,16,81]{2,1,0:T(8,128)}, f32[16,16,81]{2,1,0:T(8,128)S(1)}, u32[]{:S(2)}, u32[]{:S(2)}) collective-permute-start(f32[16,16,81]{2,1,0:T(8,128)} %get-tuple-element.12), channel_id=1, source_target_pairs={{0,496},{16,0},{32,16},{48,32},{64,48},{80,64},{96,80},{112,96},{1... | collective-permute-start | bytes 248840 | tf_op jit(solution)/shard_map/ppermute | solution.py:26
  69.9 30.7 %collective-permute-start.2 = (f32[16,16,81]{2,1,0:T(8,128)}, f32[16,16,81]{2,1,0:T(8,128)S(1)}, u32[]{:S(2)}, u32[]{:S(2)}) collective-permute-start(f32[16,16,81]{2,1,0:T(8,128)} %get-tuple-element.13), channel_id=1, source_target_pairs={{0,16},{16,32},{32,48},{48,64},{64,80},{80,96},{96,112},{112,128},... | collective-permute-start | bytes 248840 | tf_op jit(solution)/shard_map/ppermute | solution.py:26
  72.9 27.7 %collective-permute-start.3 = (f32[16,16,81]{2,1,0:T(8,128)}, f32[16,16,81]{2,1,0:T(8,128)S(1)}, u32[]{:S(2)}, u32[]{:S(2)}) collective-permute-start(f32[16,16,81]{2,1,0:T(8,128)} %get-tuple-element.14), channel_id=1, source_target_pairs={{0,32},{16,48},{32,64},{48,80},{64,96},{80,112},{96,128},{112,144}... | collective-permute-start | bytes 248840 | tf_op jit(solution)/shard_map/ppermute | solution.py:26
  92.5 15.8 %all-to-all-start = ((f32[8,8,512]{2,1,0:T(8,128)}), f32[8,8,512]{2,1,0:T(8,128)S(1)}, u32[]{:S(2)}, u32[]{:S(2)}) async-start(f32[8,8,512]{2,1,0:T(8,128)} %get-tuple-element.15), calls=%async_computation | async-start | bytes 262144 | tf_op jit(solution)/shard_map/all_to_all | solution.py:173

commit v2 on v1

v2 whole, which is shorter than its diff:
```python
import jax
import jax.numpy as jnp
import numpy as np
from jax import lax
from jax.experimental import pallas as pl
from jax.experimental.pallas import tpu as pltpu
from jax.sharding import PartitionSpec as P


BASIS = 9
POINTS = 16
SLOTS = 32
REACH = 2
G = 81
SAMPLES = 256
WINDOW = 80
LANES = 128
UNROLL = 4
VMEM_BYTES = 24 * 2**20

VMEM = pl.BlockSpec(memory_space=pltpu.VMEM)


def passed_along(value, axis, steps):
    count = lax.axis_size(axis)
    pairs = [(source, (source + steps) % count) for source in range(count)]
    return lax.ppermute(value, axis, pairs)


def exchanged(value, axis, bit):
    return lax.ppermute(value, axis, [(i, i ^ bit) for i in range(lax.axis_size(axis))])


def basis_table():
    points = np.arange(POINTS) * (2.0 * np.pi / POINTS)
    rows = [np.ones(POINTS)]
    for k in range(1, BASIS // 2 + 1):
        rows.append(np.sqrt(2.0) * np.cos(k * points))
        rows.append(np.sqrt(2.0) * np.sin(k * points))
    single = np.stack(rows).astype(np.float32)
    product = single[:, None, :, None] * single[None, :, None, :]
    return product.reshape(G, SAMPLES).astype(jnp.bfloat16)


def dot(a, b):
    return jnp.dot(a, b, preferred_element_type=jnp.float32)


def dot_nt(a, b):
    return lax.dot_general(a, b, (((1,), (1,)), ((), ())), preferred_element_type=jnp.float32)


def selector(neighbors_ref, counts_ref, block_len, edges):
    position = lax.axis_index("atom")
    atom_count = lax.axis_size("atom")
    sources = neighbors_ref[...]
    block = lax.rem(
        lax.div(sources, block_len) - position + (REACH + atom_count), jnp.int32(atom_count)
    )
    half = lax.div(block, jnp.int32(2))
    block = jnp.where(lax.rem(block, jnp.int32(2)) == 1, half + (REACH + 1), half)
    slot = (block * block_len + lax.rem(sources, block_len)).astype(jnp.bfloat16)
    edge = lax.broadcasted_iota(jnp.int32, (SLOTS, edges), 1)
    spread = (edge % SLOTS == lax.broadcasted_iota(jnp.int32, (SLOTS, edges), 0)).astype(jnp.bfloat16)
    edge = lax.broadcasted_iota(jnp.int32, (block_len, edges), 1)
    mine = edge // SLOTS == lax.broadcasted_iota(jnp.int32, (block_len, edges), 0)
    slot_row = jnp.sum(jnp.where(mine, dot(slot, spread), 0.0), axis=0, keepdims=True)
    counts = jnp.broadcast_to(counts_ref[...], (8, block_len)).astype(jnp.bfloat16)
    count_row = dot(counts, mine.astype(jnp.bfloat16))[:1]
    in_row = (lax.broadcasted_iota(jnp.int32, (1, edges), 1) % SLOTS).astype(jnp.float32)
    slot_row = jnp.where(in_row < count_row, slot_row, -1.0)
    window = lax.broadcasted_iota(jnp.int32, (WINDOW, edges), 0).astype(jnp.float32)
    return (window == slot_row).astype(jnp.bfloat16)


def split(value):
    high = value.astype(jnp.bfloat16)
    return high, (value - high.astype(jnp.float32)).astype(jnp.bfloat16)


def filter_grids(weight_ref, table_ref, grids_ref):
    for half, value in enumerate(split(dot(weight_ref[...], table_ref[...]))):
        for run in range(SAMPLES // LANES):
            part = value[:, run * LANES : (run + 1) * LANES]
            grids_ref[half, run] = part.astype(jnp.float32)


def filter_grid(grids_ref, c, degrees, chan_count):
    rows = pl.ds(c, degrees, stride=chan_count)
    halves = [
        jnp.concatenate([grids_ref[half, run, rows, :] for run in range(SAMPLES // LANES)], axis=1)
        for half in range(2)
    ]
    return jnp.concatenate(halves, axis=0)


def edge_terms(
    edge_grad_ref, weight_ref, neighbors_ref, counts_ref, radial_ref, table_ref, rows_ref,
    even_ref, odd_ref,
    weight_out, radial_out, left_out, own_out, right_out, odd_out,
    grad_ref, sel_ref, grids_ref, window_ref, moments_ref,
):
    grad_ref[...] = jnp.swapaxes(edge_grad_ref[...], 0, 1)
    chan_count, _, edges = grad_ref.shape
    degrees = radial_ref.shape[0]
    even_len = even_ref.shape[1]
    block_len = own_out.shape[1]
    sel_ref[...] = selector(neighbors_ref, counts_ref, block_len, edges)
    filter_grids(weight_ref, table_ref, grids_ref)
    window_ref[:, :even_len, :] = even_ref[...]
    first = pl.multiple_of(lax.rem(lax.axis_index("atom"), 2) * block_len, block_len)
    window_ref[:, even_len:, :] = odd_ref[:, pl.ds(first, REACH * block_len), :]
    radial = jnp.concatenate([radial_ref[...]] * 2, axis=0)

    def channel(c, total):
        weighted = dot(rows_ref[...], grad_ref[c])
        weight_grid = filter_grid(grids_ref, c, degrees, chan_count)
        filt_grid = dot(weight_grid.T.astype(jnp.bfloat16), radial)
        window_grid = dot(window_ref[c], table_ref[...]).T.astype(jnp.bfloat16)
        feat_grid = dot(window_grid, sel_ref[...])
        feat_side = (weighted * filt_grid).astype(jnp.bfloat16)
        filt_side = (weighted * feat_grid).astype(jnp.bfloat16)
        moments_ref[:, c, :] = dot_nt(radial_ref[...], filt_side)
        total = total + dot(weight_grid.astype(jnp.bfloat16), filt_side)
        window_sum = dot_nt(sel_ref[...], feat_side).astype(jnp.bfloat16)
        window_grad = dot(window_sum, rows_ref[...]) * (1.0 / SAMPLES)
        for j, out in enumerate((left_out, own_out, right_out)):
            out[c] = window_grad[j * block_len : (j + 1) * block_len, :]
        odd_out[c] = window_grad[even_len:, :]
        return total

    total = lax.fori_loop(
        0, chan_count, channel, jnp.zeros((2 * degrees, edges), jnp.float32), unroll=UNROLL
    )
    radial_sum = (total[:degrees] + total[degrees:]) * (1.0 / SAMPLES)
    for j in range(radial_out.shape[0]):
        radial_out[j] = radial_sum
    high, low = split(moments_ref[...].reshape(degrees * chan_count, SAMPLES))
    weight = dot_nt(high, table_ref[...]) + dot_nt(low, table_ref[...])
    weight_out[...] = weight * (1.0 / SAMPLES)


def stack_blocks(left_ref, own_ref, right_ref, out_ref):
    block_len = own_ref.shape[1]
    for j, ref in enumerate((left_ref, own_ref, right_ref)):
        out_ref[:, j * block_len : (j + 1) * block_len, :] = ref[...]


def pair_sums(left_ref, own_ref, right_ref, odd_ref, left_out, own_out, right_out):
    block_len = own_ref.shape[1]
    second = lax.rem(lax.axis_index("atom"), 2) == 1
    before, after = odd_ref[:, :block_len, :], odd_ref[:, block_len:, :]
    zero = jnp.zeros_like(before)
    left_out[...] = (left_ref[...] + jnp.where(second, before, zero)).astype(left_out.dtype)
    right_out[...] = (right_ref[...] + jnp.where(second, zero, after)).astype(right_out.dtype)
    own_out[...] = own_ref[...] + jnp.where(second, after, before)


def local(feats, neighbors, counts, radial, filter_weight, message_grad):
    table = basis_table()
    rows = jnp.asarray(np.ascontiguousarray(table.T))
    table = jnp.asarray(table)
    atom_count = lax.axis_size("atom")
    chan_devices = lax.axis_size("chan")
    _, chan_count, _, block_len = feats.shape
    degrees, edges = radial.shape[1:]
    params = pltpu.CompilerParams(vmem_limit_bytes=VMEM_BYTES)

    own_block = jnp.transpose(feats[0], (0, 2, 1))
    left = passed_along(own_block, "atom", REACH)
    right = passed_along(own_block, "atom", -REACH)
    even = pl.pallas_call(
        stack_blocks,
        out_shape=jax.ShapeDtypeStruct((chan_count, (REACH + 1) * block_len, G), feats.dtype),
        in_specs=[VMEM] * 3,
        out_specs=VMEM,
        compiler_params=params,
        cost_estimate=pl.CostEstimate(flops=10**9, bytes_accessed=6 * 10**7, transcendentals=0),
        name="stack_blocks",
    )(left, own_block, right)
    odd = exchanged(even, "atom", 1)

    weight = filter_weight.reshape(degrees * chan_count, G)
    block = jax.ShapeDtypeStruct((chan_count, block_len, G), jnp.float32)
    weight_part, radial_part, left, own, right, odd = pl.pallas_call(
        edge_terms,
        out_shape=(
            jax.ShapeDtypeStruct((degrees * chan_count, G), jnp.float32),
            jax.ShapeDtypeStruct((chan_devices, degrees, edges), jnp.float32),
            block,
            block,
            block,
            jax.ShapeDtypeStruct((chan_count, REACH * block_len, G), jnp.float32),
        ),
        in_specs=[VMEM] * 9,
        out_specs=(VMEM,) * 6,
        scratch_shapes=[
            pltpu.VMEM((chan_count, G, edges), jnp.bfloat16),
            pltpu.VMEM((WINDOW, edges), jnp.bfloat16),
            pltpu.VMEM((2, SAMPLES // LANES, degrees * chan_count, LANES), jnp.float32),
            pltpu.VMEM((chan_count, WINDOW, G), jnp.bfloat16),
            pltpu.VMEM((degrees, chan_count, SAMPLES), jnp.float32),
        ],
        compiler_params=params,
        cost_estimate=pl.CostEstimate(flops=10**10, bytes_accessed=4 * 10**6, transcendentals=0),
        name="edge_terms",
    )(jnp.swapaxes(message_grad[0], 0, 1), weight, neighbors[0], counts, radial[0], table, rows, even, odd)

    group = ("atom", "rep")
    members = lax.axis_size(group)
    pieces = lax.all_to_all(weight_part.reshape(members, -1, G), group, 0, 0, tiled=True)
    piece = jnp.sum(pieces, axis=0, keepdims=True) / (atom_count * block_len * lax.axis_size("rep"))
    weight_grad = lax.all_to_all(
        jnp.broadcast_to(piece, pieces.shape), group, 0, 0, tiled=True
    )
    weight_grad = weight_grad.reshape(degrees, chan_count, G)
    radial_parts = lax.all_to_all(radial_part, "chan", 0, 0, tiled=True)
    radial_grad = jnp.sum(radial_parts, axis=0, keepdims=True)

    odd = exchanged(odd, "atom", 1)
    sent = jax.ShapeDtypeStruct(block.shape, jnp.bfloat16)
    left, own, right = pl.pallas_call(
        pair_sums,
        out_shape=[sent, block, sent],
        in_specs=[VMEM] * 4,
        out_specs=[VMEM] * 3,
        compiler_params=params,
        cost_estimate=pl.CostEstimate(flops=10**6, bytes_accessed=10**6, transcendentals=0),
        name="pair_sums",
    )(left, own, right, odd)
    left = passed_along(left, "atom", -REACH)
    right = passed_along(right, "atom", REACH)
    feat_grad = own + left.astype(jnp.float32) + right.astype(jnp.float32)
    feat_grad = jnp.transpose(feat_grad, (0, 2, 1))[None]
    return (feat_grad, radial_grad, weight_grad)


def solution(mesh):
    placed = (
        P("rep", "chan", None, "atom"),
        P("rep", "atom", None),
        P("rep", "atom"),
        P("rep", None, "atom"),
        P(None, "chan", None),
        P("rep", "chan", None, "atom"),
    )

    return jax.shard_map(
        local,
        mesh=mesh,
        in_specs=placed,
        out_specs=(P("rep", "chan", None, "atom"), P("rep", None, "atom"), P(None, "chan", None)),
        check_vma=False,
    )
```

time: 110 us -> 87.7 us (0.80)
  waiting for transfers between devices: 5.5 us -> 23.2 us
  blocking collectives: 17.5 us -> 0 us
  Pallas kernels: 26.2 us -> 12.7 us
  starting transfers between devices: 50.7 us -> 46.4 us
  local copies, waits for them, and re-layouts: 5.25 us -> 2.15 us
  other arithmetic: 2.95 us -> 1.38 us
    all_to_all x1 -> x0, blocking collectives: 17.5 us -> none  [local(): lax.all_to_all(jnp.broadcast_to(piece, pieces.shape), group, 0, 0, tiled=...]
    ppermute x8 -> x4, starting transfers between devices: 35.1 us -> 19.8 us  [passed_along(): return lax.ppermute(value, axis, pairs)]
    pallas_call x2 -> x3, Pallas kernels: 26.2 us -> 12.7 us  [the longest x1 12.6 us: local(): pl.pallas_call(edge_terms, out_shape=(jax.ShapeDtypeStruct((degrees * cha...]
    all_to_all x1, waiting for transfers between devices: 0.01 us -> 7.5 us  [local(): lax.all_to_all(weight_part.reshape(members, -1, G), group, 0, 0, tiled=True)]
    ppermute x8 -> x4, waiting for transfers between devices: 0.02 us -> 7.2 us  [passed_along(): return lax.ppermute(value, axis, pairs)]
    ppermute x0 -> x2, starting transfers between devices: none -> 6.51 us  [exchanged(): lax.ppermute(value, axis, [(i, i ^ bit) for i in range(lax.axis_size(axis...]
    all_to_all x0 -> x1, starting transfers between devices: none -> 4.73 us  [local(): lax.all_to_all(jnp.broadcast_to(piece, pieces.shape), group, 0, 0, tiled=...]
    unnamed x11 -> x17, local copies, waits for them, and re-layouts: 5.23 us -> 1.5 us
  transfers between devices with their start and end apart: 10 -> 9, of which waited for: 1 -> 5; matrix products, arithmetic and copies ran while one was open for 6% -> 2% of each run, Pallas kernels for 13% -> 0%
where the time goes in v2:
time: 87.7 us; the launch traced here: 86.6 us
  starting transfers between devices  46.4 us (53%)
  waiting for transfers between devices  23.2 us (26%)
  Pallas kernels  12.7 us (14%)
  local copies, waits for them, and re-layouts  2.15 us (2%)
  other arithmetic  1.38 us (2%)
    ppermute x4, starting transfers between devices, passed_along(): return lax.ppermute(value, axis, pairs)  19.8 us
    pallas_call x1, Pallas kernels, local(): pl.pallas_call(edge_terms, out_shape=(jax.ShapeDtypeStruct((degrees * cha...  12.6 us
    all_to_all x1, starting transfers between devices, local(): radial_parts = lax.all_to_all(radial_part, 'chan', 0, 0, tiled=True)  10 us
    all_to_all x1, waiting for transfers between devices, local(): lax.all_to_all(weight_part.reshape(members, -1, G), group, 0, 0, tiled=True)  7.5 us
    ppermute x4, waiting for transfers between devices, passed_along(): return lax.ppermute(value, axis, pairs)  7.2 us
    all_to_all x1, waiting for transfers between devices, local(): radial_parts = lax.all_to_all(radial_part, 'chan', 0, 0, tiled=True)  7.06 us
    ppermute x2, starting transfers between devices, exchanged(): lax.ppermute(value, axis, [(i, i ^ bit) for i in range(lax.axis_size(axis...  6.51 us
    all_to_all x1, starting transfers between devices, local(): lax.all_to_all(weight_part.reshape(members, -1, G), group, 0, 0, tiled=True)  5.35 us
  transfers between devices with their start and end apart: 9, of which 5 were waited for; matrix products, arithmetic and copies ran while one was open for 2% of the time, Pallas kernels for 0%

profile of v2, /device:TPU:1, one launch (start us, length us, event | category | flops | bytes accessed | tf_op | source)
XLA Modules:
  0.0 86.6 jit_solution(13165001088458657395)
XLA Ops:
  0.6 0.0 copy-start.5
  0.6 0.0 copy-start
  0.7 8.4 %collective-permute-start.1 = (bf16[16,16,81]{2,1,0:T(8,128)(2,1)}, bf16[16,16,81]{2,1,0:T(8,128)(2,1)S(1)}, u32[]{:S(2)}, u32[]{:S(2)}) collective-permute-start(bf16[16,16,81]{2,1,0:T(8,128)(2,1)} %bitcast.17), channel_id=1, source_target_pairs={{0,480},{16,496},{32,0},{48,16},{64,32},{80,48},{96,64},{112,80},{... | collective-permute-start | bytes 124424 | tf_op jit(solution)/shard_map/ppermute | solution.py:27
  9.0 1.9 %collective-permute-start = (bf16[16,16,81]{2,1,0:T(8,128)(2,1)}, bf16[16,16,81]{2,1,0:T(8,128)(2,1)S(1)}, u32[]{:S(2)}, u32[]{:S(2)}) collective-permute-start(bf16[16,16,81]{2,1,0:T(8,128)(2,1)} %bitcast.18), channel_id=1, source_target_pairs={{0,32},{16,48},{32,64},{48,80},{64,96},{80,112},{96,128},{112,144}... | collective-permute-start | bytes 124424 | tf_op jit(solution)/shard_map/ppermute | solution.py:27
  11.0 0.0 collective-permute-done.1.right_ref
  11.0 7.2 %collective-permute-done.left_ref = bf16[16,16,81]{2,1,0:T(8,128)(2,1)S(1)} collective-permute-done((bf16[16,16,81]{2,1,0:T(8,128)(2,1)}, bf16[16,16,81]{2,1,0:T(8,128)(2,1)S(1)}, u32[]{:S(2)}, u32[]{:S(2)}) %collective-permute-start) | collective-permute-done | bytes 41504 | tf_op jit(solution)/shard_map/ppermute | solution.py:27
  18.2 0.0 copy-start.1
  18.2 0.8 copy-done.1
  19.0 0.0 copy-start.2
  19.0 0.0 copy-start.3
  19.0 0.0 copy-start.4
  19.0 0.0 copy-start.6
  19.0 0.0 copy-start.7
  19.1 4.1 %collective-permute-start.2 = (bf16[16,48,81]{2,1,0:T(8,128)(2,1)S(1)}, bf16[16,48,81]{2,1,0:T(8,128)(2,1)S(1)}, u32[]{:S(2)}, u32[]{:S(2)}) collective-permute-start(bf16[16,48,81]{2,1,0:T(8,128)(2,1)S(1)} %stack_blocks.1.even_ref), channel_id=1, source_target_pairs={{0,16},{16,0},{32,48},{48,32},{64,80},{80,64},{96,112},{112,96},{1... | collective-permute-start | bytes 373256 | tf_op jit(solution)/shard_map/ppermute | solution.py:31
  23.2 1.0 %collective-permute-done.2.odd_ref = bf16[16,48,81]{2,1,0:T(8,128)(2,1)S(1)} collective-permute-done((bf16[16,48,81]{2,1,0:T(8,128)(2,1)S(1)}, bf16[16,48,81]{2,1,0:T(8,128)(2,1)S(1)}, u32[]{:S(2)}, u32[]{:S(2)}) %collective-permute-start.2) | collective-permute-done | bytes 124448 | tf_op jit(solution)/shard_map/ppermute | solution.py:31
  24.3 0.0 copy-done.5
  24.3 0.0 copy-done
  24.3 0.0 copy-done.2
  24.3 0.0 copy-done.3
  24.3 0.0 copy-done.4
  24.3 0.0 copy-done.6
  24.3 0.0 copy-done.7
  24.3 12.6 %edge_terms.1 = (f32[128,81]{1,0:T(8,128)}, f32[8,8,512]{2,1,0:T(8,128)}, f32[16,16,81]{2,1,0:T(8,128)S(1)}, f32[16,16,81]{2,1,0:T(8,128)S(1)}, f32[16,16,81]{2,1,0:T(8,128)S(1)}, /*index=5*/f32[16,32,81]{2,1,0:T(8,128)S(1)}) custom-call(bf16[81,16,512]{2,1,0:T(8,128)(2,1)S(1)} %bitcast.16, bf16[128,81]{1,0:T(8,128)(2,1)S(1)} %bitcast.20, ...), custom_call_target="tpu_custom_call" | custom-call | flops 10000000000 | bytes 4000000 | tf_op jit(solution)/shard_map/edge_terms/pallas_call | solution.py:185
  36.9 5.3 %all-to-all-start.1 = ((f32[64,2,81]{2,1,0:T(2,128)}), f32[64,2,81]{2,1,0:T(2,128)S(1)}, u32[]{:S(2)}, u32[]{:S(2)}) async-start(f32[64,2,81]{2,1,0:T(2,128)} %bitcast.11), calls=%async_computation.1 | async-start | bytes 131072 | tf_op jit(solution)/shard_map/all_to_all | solution.py:211
  42.2 2.4 %collective-permute-start.3 = (f32[16,32,81]{2,1,0:T(8,128)S(1)}, f32[16,32,81]{2,1,0:T(8,128)S(1)}, u32[]{:S(2)}, u32[]{:S(2)}) collective-permute-start(f32[16,32,81]{2,1,0:T(8,128)S(1)} %get-tuple-element.15), channel_id=1, source_target_pairs={{0,16},{16,0},{32,48},{48,32},{64,80},{80,64},{96,112},{112,96},{1... | collective-permute-start | bytes 497672 | tf_op jit(solution)/shard_map/ppermute | solution.py:31
  44.6 7.5 %all-to-all-done.1 = f32[64,2,81]{2,1,0:T(2,128)S(1)} async-done(((f32[64,2,81]{2,1,0:T(2,128)}), f32[64,2,81]{2,1,0:T(2,128)S(1)}, u32[]{:S(2)}, u32[]{:S(2)}) %all-to-all-start.1) | async-done | bytes 41504 | tf_op jit(solution)/shard_map/all_to_all | solution.py:211
  52.1 0.1 reduce_sum.19
  52.2 0.7 broadcast_in_dim.14
  52.8 4.7 %all-to-all-start.2 = ((f32[64,2,81]{2,1,0:T(2,128)}), f32[64,2,81]{2,1,0:T(2,128)S(1)}, u32[]{:S(2)}, u32[]{:S(2)}) async-start(f32[64,2,81]{2,1,0:T(2,128)} %broadcast_in_dim.14), calls=%async_computation.2 | async-start | bytes 131072 | tf_op jit(solution)/shard_map/all_to_all | solution.py:213
  57.6 0.0 collective-permute-done.3.odd_ref
  57.6 0.1 pair_sums.1
  57.7 7.6 %collective-permute-start.4 = (bf16[16,16,81]{2,1,0:T(8,128)(2,1)S(1)}, bf16[16,16,81]{2,1,0:T(8,128)(2,1)S(1)}, u32[]{:S(2)}, u32[]{:S(2)}) collective-permute-start(bf16[16,16,81]{2,1,0:T(8,128)(2,1)S(1)} %get-tuple-element.17), channel_id=1, source_target_pairs={{0,480},{16,496},{32,0},{48,16},{64,32},{80,48},{96,64},{112,80},{... | collective-permute-start | bytes 124424 | tf_op jit(solution)/shard_map/ppermute | solution.py:27
  65.2 1.9 %collective-permute-start.5 = (bf16[16,16,81]{2,1,0:T(8,128)(2,1)S(1)}, bf16[16,16,81]{2,1,0:T(8,128)(2,1)S(1)}, u32[]{:S(2)}, u32[]{:S(2)}) collective-permute-start(bf16[16,16,81]{2,1,0:T(8,128)(2,1)S(1)} %get-tuple-element.18), channel_id=1, source_target_pairs={{0,32},{16,48},{32,64},{48,80},{64,96},{80,112},{96,128},{112,144}... | collective-permute-start | bytes 124424 | tf_op jit(solution)/shard_map/ppermute | solution.py:27
  67.2 0.4 all-to-all-done.2
  67.6 10.0 %all-to-all-start = ((f32[8,8,512]{2,1,0:T(8,128)}), f32[8,8,512]{2,1,0:T(8,128)S(1)}, u32[]{:S(2)}, u32[]{:S(2)}) async-start(f32[8,8,512]{2,1,0:T(8,128)} %get-tuple-element.19), calls=%async_computation | async-start | bytes 262144 | tf_op jit(solution)/shard_map/all_to_all | solution.py:217
  77.6 0.0 collective-permute-done.4
  77.6 0.0 collective-permute-done.5
  77.6 0.7 add_bitcast_fusion
  78.3 7.1 %all-to-all-done = f32[8,8,512]{2,1,0:T(8,128)S(1)} async-done(((f32[8,8,512]{2,1,0:T(8,128)}), f32[8,8,512]{2,1,0:T(8,128)S(1)}, u32[]{:S(2)}, u32[]{:S(2)}) %all-to-all-start) | async-done | bytes 131104 | tf_op jit(solution)/shard_map/all_to_all | solution.py:217
  85.4 0.6 reduce_sum.18
  86.0 0.6 copy.12
  (2 shorter events, 0.0 us)
Async XLA Ops:
  0.6 23.6 %copy-start.5 = (s32[1,16]{1,0:T(1,128)S(1)}, s32[1,16]{1,0:T(1,128)}, u32[]{:S(2)}) copy-start(s32[1,16]{1,0:T(1,128)} %counts_ref.1) | copy-start | bytes 196
  0.6 23.6 %copy-start = (bf16[1,16,81,512]{3,1,2,0:T(8,128)(2,1)S(1)}, bf16[1,16,81,512]{3,1,2,0:T(8,128)(2,1)}, u32[]{:S(2)}) copy-start(bf16[1,16,81,512]{3,1,2,0:T(8,128)(2,1)} %param.13) | copy-start | bytes 3981316
  0.7 10.3 %collective-permute-start.1 = (bf16[16,16,81]{2,1,0:T(8,128)(2,1)}, bf16[16,16,81]{2,1,0:T(8,128)(2,1)S(1)}, u32[]{:S(2)}, u32[]{:S(2)}) collective-permute-start(bf16[16,16,81]{2,1,0:T(8,128)(2,1)} %bitcast.17), channel_id=1, source_target_pairs={{0,480},{16,496},{32,0},{48,16},{64,32},{80,48},{96,64},{112,80},{... | collective-permute-start | bytes 124424 | tf_op jit(solution)/shard_map/ppermute | solution.py:27
  9.0 9.1 %collective-permute-start = (bf16[16,16,81]{2,1,0:T(8,128)(2,1)}, bf16[16,16,81]{2,1,0:T(8,128)(2,1)S(1)}, u32[]{:S(2)}, u32[]{:S(2)}) collective-permute-start(bf16[16,16,81]{2,1,0:T(8,128)(2,1)} %bitcast.18), channel_id=1, source_target_pairs={{0,32},{16,48},{32,64},{48,80},{64,96},{80,112},{96,128},{112,144}... | collective-permute-start | bytes 124424 | tf_op jit(solution)/shard_map/ppermute | solution.py:27
  18.2 0.8 copy-start.1
  19.0 5.3 %copy-start.2 = (bf16[8,16,81]{2,1,0:T(8,128)(2,1)S(1)}, bf16[8,16,81]{2,1,0:T(8,128)(2,1)}, u32[]{:S(2)}) copy-start(bf16[8,16,81]{2,1,0:T(8,128)(2,1)} %param.12) | copy-start | bytes 62212
  19.0 5.3 %copy-start.3 = (s32[1,16,32]{2,1,0:T(8,128)S(1)}, s32[1,16,32]{2,1,0:T(8,128)}, u32[]{:S(2)}) copy-start(s32[1,16,32]{2,1,0:T(8,128)} %param.9) | copy-start | bytes 6148
  19.0 5.3 %copy-start.4 = (bf16[1,8,512]{2,1,0:T(8,128)(2,1)S(1)}, bf16[1,8,512]{2,1,0:T(8,128)(2,1)}, u32[]{:S(2)}) copy-start(bf16[1,8,512]{2,1,0:T(8,128)(2,1)} %param.11) | copy-start | bytes 24580
  19.0 5.3 %copy-start.6 = (bf16[256,81]{1,0:T(8,128)(2,1)S(1)}, bf16[256,81]{1,0:T(8,128)(2,1)}, u32[]{:S(2)}) copy-start(bf16[256,81]{1,0:T(8,128)(2,1)} %constant.9.clone.rows_ref) | copy-start | bytes 124420
  19.0 5.3 %copy-start.7 = (bf16[81,256]{1,0:T(8,128)(2,1)S(1)}, bf16[81,256]{1,0:T(8,128)(2,1)}, u32[]{:S(2)}) copy-start(bf16[81,256]{1,0:T(8,128)(2,1)} %constant.10.clone.table_ref) | copy-start | bytes 124420
  19.1 5.2 %collective-permute-start.2 = (bf16[16,48,81]{2,1,0:T(8,128)(2,1)S(1)}, bf16[16,48,81]{2,1,0:T(8,128)(2,1)S(1)}, u32[]{:S(2)}, u32[]{:S(2)}) collective-permute-start(bf16[16,48,81]{2,1,0:T(8,128)(2,1)S(1)} %stack_blocks.1.even_ref), channel_id=1, source_target_pairs={{0,16},{16,0},{32,48},{48,32},{64,80},{80,64},{96,112},{112,96},{1... | collective-permute-start | bytes 373256 | tf_op jit(solution)/shard_map/ppermute | solution.py:31
  36.9 15.2 %all-to-all-start.1 = ((f32[64,2,81]{2,1,0:T(2,128)}), f32[64,2,81]{2,1,0:T(2,128)S(1)}, u32[]{:S(2)}, u32[]{:S(2)}) async-start(f32[64,2,81]{2,1,0:T(2,128)} %bitcast.11), calls=%async_computation.1 | async-start | bytes 131072 | tf_op jit(solution)/shard_map/all_to_all | solution.py:211
  42.2 15.3 %collective-permute-start.3 = (f32[16,32,81]{2,1,0:T(8,128)S(1)}, f32[16,32,81]{2,1,0:T(8,128)S(1)}, u32[]{:S(2)}, u32[]{:S(2)}) collective-permute-start(f32[16,32,81]{2,1,0:T(8,128)S(1)} %get-tuple-element.15), channel_id=1, source_target_pairs={{0,16},{16,0},{32,48},{48,32},{64,80},{80,64},{96,112},{112,96},{1... | collective-permute-start | bytes 497672 | tf_op jit(solution)/shard_map/ppermute | solution.py:31
  52.8 14.7 %all-to-all-start.2 = ((f32[64,2,81]{2,1,0:T(2,128)}), f32[64,2,81]{2,1,0:T(2,128)S(1)}, u32[]{:S(2)}, u32[]{:S(2)}) async-start(f32[64,2,81]{2,1,0:T(2,128)} %broadcast_in_dim.14), calls=%async_computation.2 | async-start | bytes 131072 | tf_op jit(solution)/shard_map/all_to_all | solution.py:213
  57.7 19.9 %collective-permute-start.4 = (bf16[16,16,81]{2,1,0:T(8,128)(2,1)S(1)}, bf16[16,16,81]{2,1,0:T(8,128)(2,1)S(1)}, u32[]{:S(2)}, u32[]{:S(2)}) collective-permute-start(bf16[16,16,81]{2,1,0:T(8,128)(2,1)S(1)} %get-tuple-element.17), channel_id=1, source_target_pairs={{0,480},{16,496},{32,0},{48,16},{64,32},{80,48},{96,64},{112,80},{... | collective-permute-start | bytes 124424 | tf_op jit(solution)/shard_map/ppermute | solution.py:27
  65.2 12.4 %collective-permute-start.5 = (bf16[16,16,81]{2,1,0:T(8,128)(2,1)S(1)}, bf16[16,16,81]{2,1,0:T(8,128)(2,1)S(1)}, u32[]{:S(2)}, u32[]{:S(2)}) collective-permute-start(bf16[16,16,81]{2,1,0:T(8,128)(2,1)S(1)} %get-tuple-element.18), channel_id=1, source_target_pairs={{0,32},{16,48},{32,64},{48,80},{64,96},{80,112},{96,128},{112,144}... | collective-permute-start | bytes 124424 | tf_op jit(solution)/shard_map/ppermute | solution.py:27
  67.6 17.8 %all-to-all-start = ((f32[8,8,512]{2,1,0:T(8,128)}), f32[8,8,512]{2,1,0:T(8,128)S(1)}, u32[]{:S(2)}, u32[]{:S(2)}) async-start(f32[8,8,512]{2,1,0:T(8,128)} %get-tuple-element.19), calls=%async_computation | async-start | bytes 262144 | tf_op jit(solution)/shard_map/all_to_all | solution.py:217

commit v3 on v2

--- a/solution.py
+++ b/solution.py
@@ -15,7 +15,7 @@
 SAMPLES = 256
 WINDOW = 80
 LANES = 128
-UNROLL = 4
+UNROLL = 8
 VMEM_BYTES = 24 * 2**20
 
 VMEM = pl.BlockSpec(memory_space=pltpu.VMEM)
@@ -133,11 +133,22 @@
         0, chan_count, channel, jnp.zeros((2 * degrees, edges), jnp.float32), unroll=UNROLL
     )
     radial_sum = (total[:degrees] + total[degrees:]) * (1.0 / SAMPLES)
+    radial_sum = radial_sum.astype(radial_out.dtype)
     for j in range(radial_out.shape[0]):
         radial_out[j] = radial_sum
     high, low = split(moments_ref[...].reshape(degrees * chan_count, SAMPLES))
     weight = dot_nt(high, table_ref[...]) + dot_nt(low, table_ref[...])
     weight_out[...] = weight * (1.0 / SAMPLES)
+
+
+def copy_block(block_ref, out_ref):
+    out_ref[...] = block_ref[...]
+
+
+def join_pieces(pieces_ref, out_ref):
+    count, length, _ = pieces_ref.shape
+    for i in range(count):
+        out_ref[i * length : (i + 1) * length, :] = pieces_ref[i]
 
 
 def stack_blocks(left_ref, own_ref, right_ref, out_ref):
@@ -169,6 +180,15 @@
     own_block = jnp.transpose(feats[0], (0, 2, 1))
     left = passed_along(own_block, "atom", REACH)
     right = passed_along(own_block, "atom", -REACH)
+    own = pl.pallas_call(
+        copy_block,
+        out_shape=jax.ShapeDtypeStruct(own_block.shape, own_block.dtype),
+        in_specs=[VMEM],
+        out_specs=VMEM,
+        compiler_params=params,
+        cost_estimate=pl.CostEstimate(flops=10**6, bytes_accessed=10**6, transcendentals=0),
+        name="copy_block",
+    )(own_block)
     even = pl.pallas_call(
         stack_blocks,
         out_shape=jax.ShapeDtypeStruct((chan_count, (REACH + 1) * block_len, G), feats.dtype),
@@ -177,7 +197,7 @@
         compiler_params=params,
         cost_estimate=pl.CostEstimate(flops=10**9, bytes_accessed=6 * 10**7, transcendentals=0),
         name="stack_blocks",
-    )(left, own_block, right)
+    )(left, own, right)
     odd = exchanged(even, "atom", 1)
 
     weight = filter_weight.reshape(degrees * chan_count, G)
@@ -186,7 +206,7 @@
         edge_terms,
         out_shape=(
             jax.ShapeDtypeStruct((degrees * chan_count, G), jnp.float32),
-            jax.ShapeDtypeStruct((chan_devices, degrees, edges), jnp.float32),
+            jax.ShapeDtypeStruct((chan_devices, degrees, edges), jnp.bfloat16),
             block,
             block,
             block,
@@ -213,9 +233,17 @@
     weight_grad = lax.all_to_all(
         jnp.broadcast_to(piece, pieces.shape), group, 0, 0, tiled=True
     )
-    weight_grad = weight_grad.reshape(degrees, chan_count, G)
+    weight_grad = pl.pallas_call(
+        join_pieces,
+        out_shape=jax.ShapeDtypeStruct((degrees * chan_count, G), jnp.float32),
+        in_specs=[VMEM],
+        out_specs=VMEM,
+        compiler_params=params,
+        cost_estimate=pl.CostEstimate(flops=10**6, bytes_accessed=10**6, transcendentals=0),
+        name="join_pieces",
+    )(weight_grad).reshape(degrees, chan_count, G)
     radial_parts = lax.all_to_all(radial_part, "chan", 0, 0, tiled=True)
-    radial_grad = jnp.sum(radial_parts, axis=0, keepdims=True)
+    radial_grad = jnp.sum(radial_parts.astype(jnp.float32), axis=0, keepdims=True)
 
     odd = exchanged(odd, "atom", 1)
     sent = jax.ShapeDtypeStruct(block.shape, jnp.bfloat16)

time: 87.7 us -> 86.8 us (0.990)
  starting transfers between devices: 46.4 us -> 43.8 us
  waiting for transfers between devices: 23.2 us -> 25.8 us
    all_to_all x1, waiting for transfers between devices: 0.38 us -> 9.25 us  [local(): lax.all_to_all(jnp.broadcast_to(piece, pieces.shape), group, 0, 0, tiled=...]
    all_to_all x1, waiting for transfers between devices: 7.06 us -> 1.78 us  [local(): radial_parts = lax.all_to_all(radial_part, 'chan', 0, 0, tiled=True)]
    ppermute x4, starting transfers between devices: 19.8 us -> 15.4 us  [passed_along(): return lax.ppermute(value, axis, pairs)]
    all_to_all x1, starting transfers between devices: 4.73 us -> 6.59 us  [local(): lax.all_to_all(jnp.broadcast_to(piece, pieces.shape), group, 0, 0, tiled=...]
    ppermute x4, waiting for transfers between devices: 7.2 us -> 6.24 us  [passed_along(): return lax.ppermute(value, axis, pairs)]
  transfers between devices with their start and end apart: 9 -> 9, of which waited for: 5 -> 5; matrix products, arithmetic and copies ran while one was open for 2% -> 2% of each run, Pallas kernels for 0% -> 1%
where the time goes in v3:
time: 86.8 us; the launch traced here: 86.3 us
  starting transfers between devices  43.8 us (50%)
  waiting for transfers between devices  25.8 us (30%)
  Pallas kernels  13 us (15%)
  local copies, waits for them, and re-layouts  1.54 us (2%)
  other arithmetic  1.38 us (2%)
    ppermute x4, starting transfers between devices, passed_along(): return lax.ppermute(value, axis, pairs)  15.4 us
    pallas_call x1, Pallas kernels, local(): pl.pallas_call(edge_terms, out_shape=(jax.ShapeDtypeStruct((degrees * cha...  12.2 us
    all_to_all x1, starting transfers between devices, local(): radial_parts = lax.all_to_all(radial_part, 'chan', 0, 0, tiled=True)  10 us
    all_to_all x1, waiting for transfers between devices, local(): lax.all_to_all(jnp.broadcast_to(piece, pieces.shape), group, 0, 0, tiled=...  9.25 us
    all_to_all x1, waiting for transfers between devices, local(): lax.all_to_all(weight_part.reshape(members, -1, G), group, 0, 0, tiled=True)  7.5 us
    all_to_all x1, starting transfers between devices, local(): lax.all_to_all(jnp.broadcast_to(piece, pieces.shape), group, 0, 0, tiled=...  6.59 us
    ppermute x2, starting transfers between devices, exchanged(): lax.ppermute(value, axis, [(i, i ^ bit) for i in range(lax.axis_size(axis...  6.38 us
    ppermute x4, waiting for transfers between devices, passed_along(): return lax.ppermute(value, axis, pairs)  6.24 us
  transfers between devices with their start and end apart: 9, of which 5 were waited for; matrix products, arithmetic and copies ran while one was open for 2% of the time, Pallas kernels for 1%

profile of v3, /device:TPU:1, one launch (start us, length us, event | category | flops | bytes accessed | tf_op | source)
XLA Modules:
  0.0 86.3 jit_solution(3457287451836696419)
XLA Ops:
  0.6 8.2 %collective-permute-start.1 = (bf16[16,16,81]{2,1,0:T(8,128)(2,1)}, bf16[16,16,81]{2,1,0:T(8,128)(2,1)S(1)}, u32[]{:S(2)}, u32[]{:S(2)}) collective-permute-start(bf16[16,16,81]{2,1,0:T(8,128)(2,1)} %bitcast.16), channel_id=1, source_target_pairs={{0,480},{16,496},{32,0},{48,16},{64,32},{80,48},{96,64},{112,80},{... | collective-permute-start | bytes 124424 | tf_op jit(solution)/shard_map/ppermute | solution.py:27
  8.9 1.9 %collective-permute-start = (bf16[16,16,81]{2,1,0:T(8,128)(2,1)}, bf16[16,16,81]{2,1,0:T(8,128)(2,1)S(1)}, u32[]{:S(2)}, u32[]{:S(2)}) collective-permute-start(bf16[16,16,81]{2,1,0:T(8,128)(2,1)} %bitcast.17), channel_id=1, source_target_pairs={{0,32},{16,48},{32,64},{48,80},{64,96},{80,112},{96,128},{112,144}... | collective-permute-start | bytes 124424 | tf_op jit(solution)/shard_map/ppermute | solution.py:27
  10.8 0.0 copy-start
  10.8 0.8 copy-done
  11.7 0.0 copy-start.1
  11.7 0.0 copy-start.2
  11.7 0.0 copy-start.3
  11.7 0.0 copy-start.4
  11.7 0.0 copy-start.5
  11.7 0.0 copy-start.6
  11.7 0.0 copy-start.7
  11.8 0.0 collective-permute-done.1.right_ref
  11.8 6.2 %collective-permute-done.left_ref = bf16[16,16,81]{2,1,0:T(8,128)(2,1)S(1)} collective-permute-done((bf16[16,16,81]{2,1,0:T(8,128)(2,1)}, bf16[16,16,81]{2,1,0:T(8,128)(2,1)S(1)}, u32[]{:S(2)}, u32[]{:S(2)}) %collective-permute-start) | collective-permute-done | bytes 41504 | tf_op jit(solution)/shard_map/ppermute | solution.py:27
  18.0 4.0 %collective-permute-start.2 = (bf16[16,48,81]{2,1,0:T(8,128)(2,1)S(1)}, bf16[16,48,81]{2,1,0:T(8,128)(2,1)S(1)}, u32[]{:S(2)}, u32[]{:S(2)}) collective-permute-start(bf16[16,48,81]{2,1,0:T(8,128)(2,1)S(1)} %stack_blocks.1.even_ref), channel_id=1, source_target_pairs={{0,16},{16,0},{32,48},{48,32},{64,80},{80,64},{96,112},{112,96},{1... | collective-permute-start | bytes 373256 | tf_op jit(solution)/shard_map/ppermute | solution.py:31
  22.1 1.0 %collective-permute-done.2.odd_ref = bf16[16,48,81]{2,1,0:T(8,128)(2,1)S(1)} collective-permute-done((bf16[16,48,81]{2,1,0:T(8,128)(2,1)S(1)}, bf16[16,48,81]{2,1,0:T(8,128)(2,1)S(1)}, u32[]{:S(2)}, u32[]{:S(2)}) %collective-permute-start.2) | collective-permute-done | bytes 124448 | tf_op jit(solution)/shard_map/ppermute | solution.py:31
  23.1 0.0 copy-done.1
  23.1 0.0 copy-done.2
  23.1 0.0 copy-done.3
  23.1 0.0 copy-done.4
  23.1 0.0 copy-done.5
  23.1 0.0 copy-done.6
  23.1 0.0 copy-done.7
  23.2 12.2 %edge_terms.1 = (f32[128,81]{1,0:T(8,128)}, bf16[8,8,512]{2,1,0:T(8,128)(2,1)}, f32[16,16,81]{2,1,0:T(8,128)S(1)}, f32[16,16,81]{2,1,0:T(8,128)S(1)}, f32[16,16,...) custom-call(bf16[81,16,512]{2,1,0:T(8,128)(2,1)S(1)} %bitcast.19, bf16[128,81]{1,0:T(8,128)(2,1)S(1)} %bitcast.20, ...), custom_call_target="tpu_custom_call" | custom-call | flops 10000000000 | bytes 4000000 | tf_op jit(solution)/shard_map/edge_terms/pallas_call | solution.py:205
  35.4 5.3 %all-to-all-start.1 = ((f32[64,2,81]{2,1,0:T(2,128)}), f32[64,2,81]{2,1,0:T(2,128)S(1)}, u32[]{:S(2)}, u32[]{:S(2)}) async-start(f32[64,2,81]{2,1,0:T(2,128)} %bitcast.11), calls=%async_computation.1 | async-start | bytes 131072 | tf_op jit(solution)/shard_map/all_to_all | solution.py:231
  40.7 2.4 %collective-permute-start.3 = (f32[16,32,81]{2,1,0:T(8,128)S(1)}, f32[16,32,81]{2,1,0:T(8,128)S(1)}, u32[]{:S(2)}, u32[]{:S(2)}) collective-permute-start(f32[16,32,81]{2,1,0:T(8,128)S(1)} %get-tuple-element.15), channel_id=1, source_target_pairs={{0,16},{16,0},{32,48},{48,32},{64,80},{80,64},{96,112},{112,96},{1... | collective-permute-start | bytes 497672 | tf_op jit(solution)/shard_map/ppermute | solution.py:31
  43.1 7.5 %all-to-all-done.1 = f32[64,2,81]{2,1,0:T(2,128)S(1)} async-done(((f32[64,2,81]{2,1,0:T(2,128)}), f32[64,2,81]{2,1,0:T(2,128)S(1)}, u32[]{:S(2)}, u32[]{:S(2)}) %all-to-all-start.1) | async-done | bytes 41504 | tf_op jit(solution)/shard_map/all_to_all | solution.py:231
  50.6 10.0 %all-to-all-start = ((bf16[8,8,512]{2,1,0:T(8,128)(2,1)}), bf16[8,8,512]{2,1,0:T(8,128)(2,1)S(1)}, u32[]{:S(2)}, u32[]{:S(2)}) async-start(bf16[8,8,512]{2,1,0:T(8,128)(2,1)} %get-tuple-element.19), calls=%async_computation | async-start | bytes 131072 | tf_op jit(solution)/shard_map/all_to_all | solution.py:245
  60.6 0.1 reduce_sum.19
  60.7 0.0 collective-permute-done.3.odd_ref
  60.7 0.1 pair_sums.1
  60.8 2.9 %collective-permute-start.4 = (bf16[16,16,81]{2,1,0:T(8,128)(2,1)S(1)}, bf16[16,16,81]{2,1,0:T(8,128)(2,1)S(1)}, u32[]{:S(2)}, u32[]{:S(2)}) collective-permute-start(bf16[16,16,81]{2,1,0:T(8,128)(2,1)S(1)} %get-tuple-element.17), channel_id=1, source_target_pairs={{0,480},{16,496},{32,0},{48,16},{64,32},{80,48},{96,64},{112,80},{... | collective-permute-start | bytes 124424 | tf_op jit(solution)/shard_map/ppermute | solution.py:27
  63.7 2.3 %collective-permute-start.5 = (bf16[16,16,81]{2,1,0:T(8,128)(2,1)S(1)}, bf16[16,16,81]{2,1,0:T(8,128)(2,1)S(1)}, u32[]{:S(2)}, u32[]{:S(2)}) collective-permute-start(bf16[16,16,81]{2,1,0:T(8,128)(2,1)S(1)} %get-tuple-element.18), channel_id=1, source_target_pairs={{0,32},{16,48},{32,64},{48,80},{64,96},{80,112},{96,128},{112,144}... | collective-permute-start | bytes 124424 | tf_op jit(solution)/shard_map/ppermute | solution.py:27
  66.1 1.8 %all-to-all-done = bf16[8,8,512]{2,1,0:T(8,128)(2,1)S(1)} async-done(((bf16[8,8,512]{2,1,0:T(8,128)(2,1)}), bf16[8,8,512]{2,1,0:T(8,128)(2,1)S(1)}, u32[]{:S(2)}, u32[]{:S(2)}) %all-to-all-start) | async-done | bytes 65568 | tf_op jit(solution)/shard_map/all_to_all | solution.py:245
  67.9 0.6 broadcast_in_dim.14
  68.5 6.6 %all-to-all-start.2 = ((f32[64,2,81]{2,1,0:T(2,128)}), f32[64,2,81]{2,1,0:T(2,128)S(1)}, u32[]{:S(2)}, u32[]{:S(2)}) async-start(f32[64,2,81]{2,1,0:T(2,128)} %broadcast_in_dim.14), calls=%async_computation.2 | async-start | bytes 131072 | tf_op jit(solution)/shard_map/all_to_all | solution.py:233
  75.1 0.6 convert_reduce_fusion
  75.7 9.3 %all-to-all-done.2.pieces_ref = f32[64,2,81]{2,1,0:T(2,128)S(1)} async-done(((f32[64,2,81]{2,1,0:T(2,128)}), f32[64,2,81]{2,1,0:T(2,128)S(1)}, u32[]{:S(2)}, u32[]{:S(2)}) %all-to-all-start.2) | async-done | bytes 41504 | tf_op jit(solution)/shard_map/all_to_all | solution.py:233
  85.0 0.7 join_pieces.1
  85.6 0.0 collective-permute-done.4
  85.6 0.0 collective-permute-done.5
  85.6 0.7 add_bitcast_fusion
  (3 shorter events, 0.1 us)
Async XLA Ops:
  0.6 11.1 %collective-permute-start.1 = (bf16[16,16,81]{2,1,0:T(8,128)(2,1)}, bf16[16,16,81]{2,1,0:T(8,128)(2,1)S(1)}, u32[]{:S(2)}, u32[]{:S(2)}) collective-permute-start(bf16[16,16,81]{2,1,0:T(8,128)(2,1)} %bitcast.16), channel_id=1, source_target_pairs={{0,480},{16,496},{32,0},{48,16},{64,32},{80,48},{96,64},{112,80},{... | collective-permute-start | bytes 124424 | tf_op jit(solution)/shard_map/ppermute | solution.py:27
  8.9 9.1 %collective-permute-start = (bf16[16,16,81]{2,1,0:T(8,128)(2,1)}, bf16[16,16,81]{2,1,0:T(8,128)(2,1)S(1)}, u32[]{:S(2)}, u32[]{:S(2)}) collective-permute-start(bf16[16,16,81]{2,1,0:T(8,128)(2,1)} %bitcast.17), channel_id=1, source_target_pairs={{0,32},{16,48},{32,64},{48,80},{64,96},{80,112},{96,128},{112,144}... | collective-permute-start | bytes 124424 | tf_op jit(solution)/shard_map/ppermute | solution.py:27
  10.8 0.9 copy-start
  11.7 11.4 %copy-start.1 = (bf16[1,16,81,512]{3,1,2,0:T(8,128)(2,1)S(1)}, bf16[1,16,81,512]{3,1,2,0:T(8,128)(2,1)}, u32[]{:S(2)}) copy-start(bf16[1,16,81,512]{3,1,2,0:T(8,128)(2,1)} %param.13) | copy-start | bytes 3981316
  11.7 11.4 %copy-start.2 = (bf16[8,16,81]{2,1,0:T(8,128)(2,1)S(1)}, bf16[8,16,81]{2,1,0:T(8,128)(2,1)}, u32[]{:S(2)}) copy-start(bf16[8,16,81]{2,1,0:T(8,128)(2,1)} %param.12) | copy-start | bytes 62212
  11.7 11.4 %copy-start.3 = (s32[1,16,32]{2,1,0:T(8,128)S(1)}, s32[1,16,32]{2,1,0:T(8,128)}, u32[]{:S(2)}) copy-start(s32[1,16,32]{2,1,0:T(8,128)} %param.9) | copy-start | bytes 6148
  11.7 11.4 %copy-start.4 = (bf16[1,8,512]{2,1,0:T(8,128)(2,1)S(1)}, bf16[1,8,512]{2,1,0:T(8,128)(2,1)}, u32[]{:S(2)}) copy-start(bf16[1,8,512]{2,1,0:T(8,128)(2,1)} %param.11) | copy-start | bytes 24580
  11.7 11.4 %copy-start.5 = (s32[1,16]{1,0:T(1,128)S(1)}, s32[1,16]{1,0:T(1,128)}, u32[]{:S(2)}) copy-start(s32[1,16]{1,0:T(1,128)} %counts_ref.1) | copy-start | bytes 196
  11.7 11.4 %copy-start.6 = (bf16[256,81]{1,0:T(8,128)(2,1)S(1)}, bf16[256,81]{1,0:T(8,128)(2,1)}, u32[]{:S(2)}) copy-start(bf16[256,81]{1,0:T(8,128)(2,1)} %constant.9.clone.rows_ref) | copy-start | bytes 124420
  11.7 11.4 %copy-start.7 = (bf16[81,256]{1,0:T(8,128)(2,1)S(1)}, bf16[81,256]{1,0:T(8,128)(2,1)}, u32[]{:S(2)}) copy-start(bf16[81,256]{1,0:T(8,128)(2,1)} %constant.10.clone.table_ref) | copy-start | bytes 124420
  18.0 5.1 %collective-permute-start.2 = (bf16[16,48,81]{2,1,0:T(8,128)(2,1)S(1)}, bf16[16,48,81]{2,1,0:T(8,128)(2,1)S(1)}, u32[]{:S(2)}, u32[]{:S(2)}) collective-permute-start(bf16[16,48,81]{2,1,0:T(8,128)(2,1)S(1)} %stack_blocks.1.even_ref), channel_id=1, source_target_pairs={{0,16},{16,0},{32,48},{48,32},{64,80},{80,64},{96,112},{112,96},{1... | collective-permute-start | bytes 373256 | tf_op jit(solution)/shard_map/ppermute | solution.py:31
  35.4 15.2 %all-to-all-start.1 = ((f32[64,2,81]{2,1,0:T(2,128)}), f32[64,2,81]{2,1,0:T(2,128)S(1)}, u32[]{:S(2)}, u32[]{:S(2)}) async-start(f32[64,2,81]{2,1,0:T(2,128)} %bitcast.11), calls=%async_computation.1 | async-start | bytes 131072 | tf_op jit(solution)/shard_map/all_to_all | solution.py:231
  40.7 20.0 %collective-permute-start.3 = (f32[16,32,81]{2,1,0:T(8,128)S(1)}, f32[16,32,81]{2,1,0:T(8,128)S(1)}, u32[]{:S(2)}, u32[]{:S(2)}) collective-permute-start(f32[16,32,81]{2,1,0:T(8,128)S(1)} %get-tuple-element.15), channel_id=1, source_target_pairs={{0,16},{16,0},{32,48},{48,32},{64,80},{80,64},{96,112},{112,96},{1... | collective-permute-start | bytes 497672 | tf_op jit(solution)/shard_map/ppermute | solution.py:31
  50.6 17.3 %all-to-all-start = ((bf16[8,8,512]{2,1,0:T(8,128)(2,1)}), bf16[8,8,512]{2,1,0:T(8,128)(2,1)S(1)}, u32[]{:S(2)}, u32[]{:S(2)}) async-start(bf16[8,8,512]{2,1,0:T(8,128)(2,1)} %get-tuple-element.19), calls=%async_computation | async-start | bytes 131072 | tf_op jit(solution)/shard_map/all_to_all | solution.py:245
  60.8 24.8 %collective-permute-start.4 = (bf16[16,16,81]{2,1,0:T(8,128)(2,1)S(1)}, bf16[16,16,81]{2,1,0:T(8,128)(2,1)S(1)}, u32[]{:S(2)}, u32[]{:S(2)}) collective-permute-start(bf16[16,16,81]{2,1,0:T(8,128)(2,1)S(1)} %get-tuple-element.17), channel_id=1, source_target_pairs={{0,480},{16,496},{32,0},{48,16},{64,32},{80,48},{96,64},{112,80},{... | collective-permute-start | bytes 124424 | tf_op jit(solution)/shard_map/ppermute | solution.py:27
  63.7 21.9 %collective-permute-start.5 = (bf16[16,16,81]{2,1,0:T(8,128)(2,1)S(1)}, bf16[16,16,81]{2,1,0:T(8,128)(2,1)S(1)}, u32[]{:S(2)}, u32[]{:S(2)}) collective-permute-start(bf16[16,16,81]{2,1,0:T(8,128)(2,1)S(1)} %get-tuple-element.18), channel_id=1, source_target_pairs={{0,32},{16,48},{32,64},{48,80},{64,96},{80,112},{96,128},{112,144}... | collective-permute-start | bytes 124424 | tf_op jit(solution)/shard_map/ppermute | solution.py:27
  68.5 16.5 %all-to-all-start.2 = ((f32[64,2,81]{2,1,0:T(2,128)}), f32[64,2,81]{2,1,0:T(2,128)S(1)}, u32[]{:S(2)}, u32[]{:S(2)}) async-start(f32[64,2,81]{2,1,0:T(2,128)} %broadcast_in_dim.14), calls=%async_computation.2 | async-start | bytes 131072 | tf_op jit(solution)/shard_map/all_to_all | solution.py:233
